TPU v7x, 128 devices: a whole 4x4x4 slice. The times are simulated.
128 devices in a mesh: ctx: 16 (over z, y), head: 8 (over x, core).
Axes of the slice: x: 4, y: 4, z: 4, core: 2. Of those that a mesh axis runs over, the one named last changes fastest.
Arguments:
- queries: bfloat16 [8192, 4096], P('ctx', 'head'), may hold values from -160 to 160
- key_states: bfloat16 [8192, 4096], P('ctx', 'head'), may hold values from -160 to 160
- values: bfloat16 [8192, 4096], P('ctx', 'head'), may hold values from -6 to 6
- query_gain: bfloat16 [4096], P('head'), may hold values from 0.25 to 1.75
- key_gain: bfloat16 [4096], P('head'), may hold values from 0.25 to 1.75
- memory_blocks: int32 [16, 8], replicated, may hold values from 0 to 63, as said below
- cotangent: bfloat16 [8192, 4096], P('ctx', 'head'), may hold values from -6 to 6
Outputs:
- attended: bfloat16 [8192, 4096], P('ctx', 'head')
- query_grads: bfloat16 [8192, 4096], P('ctx', 'head')
- key_grads: bfloat16 [8192, 4096], P('ctx', 'head')
- value_grads: bfloat16 [8192, 4096], P('ctx', 'head')
Inputs may be any that keep to these rules, and one draw needn't show every extreme that they name: `memory_blocks`: row c lists the 8 blocks read by the tokens of ctx index c; block b holds tokens 128 b to 128 b + 127, and the 8 blocks of one row lie on 8 different ctx indices.
All inputs are finite; a program needn't handle non-finite values.
Results may differ from a plain program's by a relative error of at most 0.0045.
The roundings to bfloat16 on the way count: a program that leaves them out, or rounds other values in their place, can miss the bound.
Values may be sent and summed in bfloat16 or wider, within the bound.
No kernel may reach another device: no remote copies, remote signals or barrier semaphores. Data moves between devices by JAX's collectives and lax.ppermute only.
A program may use at most 128 MiB of HBM per device.

v0:
```python
import math

import jax
import jax.numpy as jnp
from jax import lax
from jax.experimental import pallas as pl
from jax.experimental.pallas import tpu as pltpu
from jax.sharding import Mesh
from jax.sharding import PartitionSpec as P

DH = 128
D = 4096
SEG = 512
EPSILON = 1e-06
FLOOR = -1e30
SCALE = 1.0 / math.sqrt(DH)
F32 = jnp.float32
BF16 = jnp.bfloat16


def nt(a, b):
    return lax.dot_general(a, b, (((1,), (1,)), ((), ())), preferred_element_type=F32)


def nn(a, b):
    return lax.dot_general(a, b, (((1,), (0,)), ((), ())), preferred_element_type=F32)


def tn(a, b):
    return lax.dot_general(a, b, (((0,), (0,)), ((), ())), preferred_element_type=F32)


def order_matrix(transposed):
    row = lax.broadcasted_iota(jnp.int32, (SEG, SEG), 1 if transposed else 0)
    col = lax.broadcasted_iota(jnp.int32, (SEG, SEG), 0 if transposed else 1)
    rb = row >> 6
    residue = ((rb & 1) << 2) | (rb & 2) | (rb >> 2)
    return (col == ((row & 63) * 8 + residue)).astype(F32).astype(BF16)


def slab(index):
    return pl.ds(pl.multiple_of(index * DH, DH), DH)


SMEM = pl.BlockSpec(memory_space=pltpu.SMEM)
VM = pl.BlockSpec(memory_space=pltpu.VMEM)


def call(body, ins, smem, outs, scratch=(), flops=0, name=None):
    return pl.pallas_call(
        body,
        out_shape=outs,
        in_specs=[SMEM] * smem + [VM] * (len(ins) - smem),
        out_specs=jax.tree.map(lambda _: VM, outs),
        scratch_shapes=list(scratch),
        compiler_params=pltpu.CompilerParams(vmem_limit_bytes=56 << 20),
        cost_estimate=pl.CostEstimate(flops=flops, transcendentals=0, bytes_accessed=4 << 20),
        name=name,
    )(*ins)


def S(shape, dtype):
    return jax.ShapeDtypeStruct(shape, dtype)


def prep_kernel(ids, q, k, v, g, kv_out, qg_out, sums_out):
    y = ids[1]
    order = order_matrix(False)
    squares = []
    for ref in (q, k):
        x = ref[...].astype(F32)
        squares.append(jnp.sum(x * x, axis=1, keepdims=True))
    lanes = lax.broadcasted_iota(jnp.int32, (SEG, DH), 1)
    both = jnp.where(lanes == 0, squares[0], 0.0) + jnp.where(lanes == 1, squares[1], 0.0)
    hi = both.astype(BF16)
    rest = both - hi.astype(F32)
    mid = rest.astype(BF16)
    low = (rest - mid.astype(F32)).astype(BF16)
    moved = nn(order, hi) + nn(order, mid) + nn(order, low)
    sums_out[...] = jnp.transpose(moved)[0:8]
    for out, index, ref in ((kv_out, 0, k), (kv_out, 1, v), (qg_out, 0, q), (qg_out, 1, g)):
        for s in range(4):
            part = ref[:, slab((y + s) % 4)]
            out[s, index] = nn(order, part).astype(BF16)


def inverse_rows(stats, which):
    rows = []
    for c in range(4):
        total = stats[8 * c, which : which + 1]
        for h in range(1, 8):
            total = total + stats[8 * c + h, which : which + 1]
        rows.append(lax.rsqrt(total / D + EPSILON))
    return rows


def normed(raw, inverse, gain):
    t = jnp.transpose(raw.astype(F32)) * inverse * gain
    return jnp.transpose(t).astype(BF16)


def place_v_kernel(ids, p0, p1, p2, p3, out):
    y = ids[1]
    for s, piece in enumerate((p0, p1, p2, p3)):
        out[(y + 4 - s) % 4] = piece[1].reshape(4, 128, DH)


def norm_k_kernel(ids, p0, p1, p2, p3, stats, gain, out):
    y = ids[1]
    inv = jnp.concatenate(inverse_rows(stats, 1), axis=0)
    keep = lax.broadcasted_iota(jnp.int32, (4, SEG), 0)
    for s, piece in enumerate((p0, p1, p2, p3)):
        c = (y + 4 - s) % 4
        row = jnp.sum(jnp.where(keep == c, inv, 0.0), axis=0, keepdims=True)
        out[c] = normed(piece[0], row, gain[...]).reshape(4, 128, DH)


def norm_q_kernel(ids, p0, p1, p2, p3, stats, gain, q_out, g_out):
    y = ids[1]
    inv = jnp.concatenate(inverse_rows(stats, 0), axis=0)
    keep = lax.broadcasted_iota(jnp.int32, (4, SEG), 0)
    for s, piece in enumerate((p0, p1, p2, p3)):
        c = (y + 4 - s) % 4
        row = jnp.sum(jnp.where(keep == c, inv, 0.0), axis=0, keepdims=True)
        q_out[c] = normed(piece[0], row, gain[...]).reshape(4, 128, DH)
        g_out[c] = piece[1].reshape(4, 128, DH)


def head_bits(ids):
    h = 4 * ids[2] + ids[1]
    par = h & 1
    return par, 2 * par + ((h >> 1) & 1), (h >> 2) & 1


def forward_part(keys, vals, q, score_ref, mask=None):
    count = len(keys)
    top = None
    for j in range(count):
        s = nt(keys[j](), q) * SCALE
        score_ref[j] = s
        t = jnp.max(s, axis=0, keepdims=True)
        top = t if top is None else jnp.maximum(top, t)
    if mask is not None:
        top = jnp.where(mask, top, FLOOR)
    total, summed = None, None
    for j in range(count):
        w = jnp.exp(score_ref[j] - top)
        if mask is not None:
            w = jnp.where(mask, w, 0.0)
        score_ref[j] = w
        t = jnp.sum(w, axis=0, keepdims=True)
        a = tn(vals[j](), w.astype(BF16))
        total = t if total is None else total + t
        summed = a if summed is None else summed + a
    return top, total, summed


def merge(m_ref, l_ref, a_ref, at, top, total, summed):
    m = m_ref[at]
    new = jnp.maximum(m, top)
    old_f = jnp.exp(m - new)
    new_f = jnp.exp(top - new)
    m_ref[at] = new
    l_ref[at] = old_f * l_ref[at] + new_f * total
    a_ref[at] = old_f * a_ref[at] + new_f * summed


def cut(x, b):
    return x[:, b * 128 : (b + 1) * 128]


def level_forward_kernel(ids, q, k, v, m_out, l_out, a_out, score):
    par, quarter, _ = head_bits(ids)

    def level0(c, carry):
        top, total, summed = forward_part(
            [lambda j=j: k[c, j] for j in range(4)],
            [lambda j=j: v[c, j] for j in range(4)],
            q[c].reshape(SEG, DH),
            score,
        )
        for b in range(4):
            m_out[c, b] = cut(top, b)
            l_out[c, b] = cut(total, b)
            a_out[c, b] = cut(summed, b)
        return carry

    lax.fori_loop(0, 4, level0, 0)

    def level1(s, carry):
        spots = [(2 * s + i // 2, 2 * par + i % 2) for i in range(4)]
        rows = jnp.concatenate([q[c, b] for c, b in spots], axis=0)
        top, total, summed = forward_part(
            [lambda c=c, b=b: k[c, b] for c, b in spots],
            [lambda c=c, b=b: v[c, b] for c, b in spots],
            rows,
            score,
        )
        for i, at in enumerate(spots):
            merge(m_out, l_out, a_out, at, cut(top, i), cut(total, i), cut(summed, i))
        return carry

    lax.fori_loop(0, 2, level1, 0)
    spots = [(i, quarter) for i in range(4)]
    rows = jnp.concatenate([q[c, b] for c, b in spots], axis=0)
    top, total, summed = forward_part(
        [lambda c=c, b=b: k[c, b] for c, b in spots],
        [lambda c=c, b=b: v[c, b] for c, b in spots],
        rows,
        score,
    )
    for i, at in enumerate(spots):
        merge(m_out, l_out, a_out, at, cut(top, i), cut(total, i), cut(summed, i))


def backward_chunk(w, factor, key, val, q, g, delta):
    soft = w if factor is None else w * factor
    grad_soft = nt(val, g)
    grad = (soft * (grad_soft - delta)).astype(BF16)
    grad_q = tn(key, grad)
    grad_k = nn(grad, q) * SCALE
    grad_v = nn(soft.astype(BF16), g)
    return grad_q, grad_k, grad_v


def main_kernel(
    ids, lists, q, g, k0, v0, k1, v1, k2, v2, k3, v3, m_in, l_in, a_in,
    att_out, dq_out, lse_out, delta_out, send1, send2, send3, dk_own, dv_own,
    kall, vall, dk, dv, score, score3, m, l, a,
):
    z, y = ids[0], ids[1]
    par, quarter, half = head_bits(ids)
    for i, (kk, vv) in enumerate(((k0, v0), (k1, v1), (k2, v2), (k3, v3))):
        kall[i] = kk[...]
        vall[i] = vv[...]
        dk[i] = jnp.zeros((4, 4, 128, DH), F32)
        dv[i] = jnp.zeros((4, 4, 128, DH), F32)
    m[...] = m_in[...]
    l[...] = l_in[...]
    a[...] = a_in[...]

    partner = jnp.where(z % 2 == 0, 1, 3)
    halves = pl.ds(pl.multiple_of(half * 64, 64), 64)
    rels = (0, 0, partner, partner)
    mask = (lax.broadcasted_iota(jnp.int32, (1, SEG), 1) % 128) // 64 == half

    def pair(ref, j):
        c = 2 * (j % 2)
        return jnp.concatenate([ref[rels[j], c, quarter, halves], ref[rels[j], c + 1, quarter, halves]], axis=0)

    q3 = jnp.concatenate([q[c, quarter] for c in range(4)], axis=0)
    g3 = jnp.concatenate([g[c, quarter] for c in range(4)], axis=0)
    top3, total, summed = forward_part(
        [lambda j=j: pair(kall, j) for j in range(4)],
        [lambda j=j: pair(vall, j) for j in range(4)],
        q3,
        score3,
        mask,
    )
    for i in range(4):
        merge(m, l, a, (i, quarter), cut(top3, i), cut(total, i), cut(summed, i))

    def place(c, j):
        block = lists[4 * z + c, j]
        owner = block // 4
        return ((owner // 4) + 4 - z) % 4, owner % 4, block % 4

    def runs(lb):
        return [
            (rb // 2, pl.ds(pl.multiple_of((rb % 2) * 64 + lb * 16, 16), 16)) for rb in range(8)
        ]

    def load(ref, c, j):
        rel, cc, lb = place(c, j)
        return jnp.concatenate([ref[rel, cc, b, r] for b, r in runs(lb)], axis=0)

    def add(ref, c, j, term):
        rel, cc, lb = place(c, j)
        for i, (b, r) in enumerate(runs(lb)):
            ref[rel, cc, b, r] = ref[rel, cc, b, r] + term[16 * i : 16 * (i + 1)]

    def one_ctx(c, carry):
        rows = q[c].reshape(SEG, DH)
        grows = g[c].reshape(SEG, DH)
        top, total, summed = forward_part(
            [lambda j=j: load(kall, c, j) for j in range(8)],
            [lambda j=j: load(vall, c, j) for j in range(8)],
            rows,
            score,
        )
        for b in range(4):
            merge(m, l, a, (c, b), cut(top, b), cut(total, b), cut(summed, b))
        joint = jnp.concatenate([m[c, b] for b in range(4)], axis=1)
        whole = jnp.concatenate([l[c, b] for b in range(4)], axis=1)
        merged = jnp.concatenate([a[c, b] for b in range(4)], axis=1) / whole
        lse = joint + jnp.log(whole)
        delta = jnp.sum(jnp.transpose(grows.astype(F32)) * merged, axis=0, keepdims=True)
        att_out[(c + 4 - y) % 4] = jnp.transpose(merged).astype(BF16)
        lse_out[c] = lse
        delta_out[c] = delta
        factor = jnp.exp(top - lse)
        grad_q = None
        for j in range(8):
            gq, gk, gv = backward_chunk(
                score[j], factor, load(kall, c, j), load(vall, c, j), rows, grows, delta
            )
            grad_q = gq if grad_q is None else grad_q + gq
            add(dk, c, j, gk.astype(BF16).astype(F32))
            add(dv, c, j, gv.astype(BF16).astype(F32))
        grad_q = grad_q * SCALE
        for b in range(4):
            dq_out[c, b] = cut(grad_q, b)
        return carry

    lax.fori_loop(0, 4, one_ctx, 0)

    def take(ref):
        row = [cut(ref[c], b) for c in range(4) for b in range(4)]
        return row

    def pick(ref):
        parts = []
        for c in range(4):
            out = cut(ref[c], 0)
            for b in range(1, 4):
                out = jnp.where(quarter == b, cut(ref[c], b), out)
            parts.append(out)
        return jnp.concatenate(parts, axis=1)

    lse3, delta3 = pick(lse_out), pick(delta_out)
    factor3 = jnp.exp(top3 - lse3)
    grad_q = None
    for j in range(4):
        gq, gk, gv = backward_chunk(score3[j], factor3, pair(kall, j), pair(vall, j), q3, g3, delta3)
        grad_q = gq if grad_q is None else grad_q + gq
        c = 2 * (j % 2)
        for i in range(2):
            at = (rels[j], c + i, quarter, halves)
            dk[at] = dk[at] + gk[64 * i : 64 * (i + 1)]
            dv[at] = dv[at] + gv[64 * i : 64 * (i + 1)]
    for i in range(4):
        dq_out[i, quarter] = dq_out[i, quarter] + cut(grad_q, i) * SCALE
    for rel, out in ((1, send1), (2, send2), (3, send3)):
        out[0] = dk[rel].astype(BF16)
        out[1] = dv[rel].astype(BF16)
    dk_own[...] = dk[0]
    dv_own[...] = dv[0]


def level_backward_kernel(
    ids, q, g, k, v, lse, delta, dq_in, dk_in, dv_in, p0, p1, p2, p3, gain, dk, dv, adj_out, raw_out, s_out, dq,
):
    y = ids[1]
    par, quarter, _ = head_bits(ids)
    dq[...] = dq_in[...]
    dk[...] = dk_in[...]
    dv[...] = dv_in[...]

    def row(ref, c, b):
        out = cut(ref[c], 0)
        for i in range(1, 4):
            out = jnp.where(b == i, cut(ref[c], i), out)
        return out

    def part(spots, rows, grows, logs, deltas):
        grad_q = None
        for c, b in spots:
            s = nt(k[c, b], rows) * SCALE
            soft = jnp.exp(s - logs)
            gq, gk, gv = backward_chunk(soft, None, k[c, b], v[c, b], rows, grows, deltas)
            grad_q = gq if grad_q is None else grad_q + gq
            dk[c, b] = dk[c, b] + gk
            dv[c, b] = dv[c, b] + gv
        grad_q = grad_q * SCALE
        for i, (c, b) in enumerate(spots):
            dq[c, b] = dq[c, b] + cut(grad_q, i)

    def gather(spots):
        return (
            jnp.concatenate([q[c, b] for c, b in spots], axis=0),
            jnp.concatenate([g[c, b] for c, b in spots], axis=0),
            jnp.concatenate([row(lse, c, b) for c, b in spots], axis=1),
            jnp.concatenate([row(delta, c, b) for c, b in spots], axis=1),
        )

    def level0(c, carry):
        part([(c, b) for b in range(4)], q[c].reshape(SEG, DH), g[c].reshape(SEG, DH), lse[c], delta[c])
        return carry

    lax.fori_loop(0, 4, level0, 0)

    def level1(s, carry):
        spots = [(2 * s + i // 2, 2 * par + i % 2) for i in range(4)]
        part(spots, *gather(spots))
        return carry

    lax.fori_loop(0, 2, level1, 0)
    spots = [(i, quarter) for i in range(4)]
    part(spots, *gather(spots))
    for s, piece in enumerate((p0, p1, p2, p3)):
        c = (y + 4 - s) % 4
        raw = jnp.transpose(piece[0].astype(F32))
        adj = jnp.concatenate([dq[c, b] for b in range(4)], axis=1) * gain[...]
        adj_out[c] = adj
        raw_out[c] = raw
        s_out[c] = jnp.sum(raw * adj, axis=0, keepdims=True)


def final_rows(inner, stats, which, adj, raw, y, out):
    inv = jnp.concatenate(inverse_rows(stats, which), axis=0)
    for c in range(4):
        total = inner[0, c : c + 1]
        for i in range(1, 32):
            total = total + inner[i, c : c + 1]
        r = inv[c : c + 1]
        grads = r * adj[c] - raw[c] * (r * r * r) * total / D
        out[(c + 4 - y) % 4] = jnp.transpose(grads).astype(BF16)


def final_q_kernel(ids, inner, stats, adj, raw, out):
    final_rows(inner, stats, 0, adj, raw, ids[1], out)


def collect_kernel(ids, dk, dv, r1, r2, r3, p0, p1, p2, p3, gain, dv_out, adj_out, raw_out, s_out):
    y = ids[1]
    for s, piece in enumerate((p0, p1, p2, p3)):
        c = (y + 4 - s) % 4
        sums = []
        for i, own in enumerate((dk, dv)):
            total = own[c]
            for r in (r1, r2, r3):
                total = total + r[i, c].astype(F32)
            sums.append(total.reshape(SEG, DH))
        dv_out[(c + 4 - y) % 4] = sums[1].astype(BF16)
        raw = jnp.transpose(piece[0].astype(F32))
        adj = jnp.transpose(sums[0]) * gain[...]
        adj_out[c] = adj
        raw_out[c] = raw
        s_out[c] = jnp.sum(raw * adj, axis=0, keepdims=True)


def final_k_kernel(ids, inner, stats, adj, raw, out):
    final_rows(inner, stats, 1, adj, raw, ids[1], out)


def restore_kernel(ids, *refs):
    y = ids[1]
    order = order_matrix(True)
    count = len(refs) // 5
    outs = refs[4 * count :]
    for n in range(count):
        for s in range(4):
            piece = refs[4 * n + s][...]
            outs[n][:, slab((y + 4 - s) % 4)] = nn(order, piece).astype(BF16)


def shift(value, axis, step):
    return lax.ppermute(value, axis, [(i, (i + step) % 4) for i in range(4)])


def y_exchange(slots):
    return [slots[0], shift(slots[1], "y", 1), shift(slots[2], "y", 2), shift(slots[3], "y", -1)]


def y_return(slots):
    return y_exchange(slots)


def to_all(value):
    copies = jnp.broadcast_to(value, (32, *value.shape))
    return lax.all_to_all(copies, ("y", "head"), split_axis=0, concat_axis=0, tiled=True)


def shards(queries, key_states, values, query_gain, key_gain, memory_blocks, cotangent):
    z, y, hd = lax.axis_index("z"), lax.axis_index("y"), lax.axis_index("head")
    ids = jnp.stack([z, y, hd]).astype(jnp.int32)

    def gain_of(gain):
        own = lax.dynamic_index_in_dim(gain.reshape(4, DH), y, 0, keepdims=False)
        return own.astype(F32)[:, None]

    q_gain, k_gain = gain_of(query_gain), gain_of(key_gain)
    head4 = (4, 4, 128, DH)
    kv, qg, sums = call(
        prep_kernel,
        (ids, queries, key_states, values, cotangent),
        1,
        (S((4, 2, SEG, DH), BF16), S((4, 2, SEG, DH), BF16), S((8, SEG), F32)),
        flops=4 * 2 * SEG**3,
        name="prep",
    )
    kv_pieces = y_exchange(kv)
    stats = to_all(sums[:2])
    qg_pieces = y_exchange(qg)
    v0 = call(place_v_kernel, (ids, *kv_pieces), 1, S(head4, BF16), name="place_v")
    v3, v1 = shift(v0, "z", 1), shift(v0, "z", -1)
    k0 = call(norm_k_kernel, (ids, *kv_pieces, stats, k_gain), 1, S(head4, BF16), name="norm_k")
    k3, k1 = shift(k0, "z", 1), shift(k0, "z", -1)
    v2, k2 = shift(v1, "z", -1), shift(k3, "z", 1)
    q, g = call(
        norm_q_kernel,
        (ids, *qg_pieces, stats, q_gain),
        1,
        (S(head4, BF16), S(head4, BF16)),
        name="norm_q",
    )
    row4 = S((4, 4, 1, 128), F32)
    m, l, a = call(
        level_forward_kernel,
        (ids, q, k0, v0),
        1,
        (row4, row4, S(head4, F32)),
        [pltpu.VMEM((4, 128, SEG), F32)],
        flops=7 * 2 * 2 * 512 * 512 * 128,
        name="level_forward",
    )
    row = S((4, 1, SEG), F32)
    send = S((2, *head4), BF16)
    att, dq, lse, delta, send1, send2, send3, dk, dv = call(
        main_kernel,
        (ids, memory_blocks, q, g, k0, v0, k1, v1, k2, v2, k3, v3, m, l, a),
        2,
        (S((4, SEG, DH), BF16), S(head4, F32), row, row, send, send, send, S(head4, F32), S(head4, F32)),
        [
            pltpu.VMEM((4, *head4), BF16),
            pltpu.VMEM((4, *head4), BF16),
            pltpu.VMEM((4, *head4), F32),
            pltpu.VMEM((4, *head4), F32),
            pltpu.VMEM((8, 128, SEG), F32),
            pltpu.VMEM((4, 128, SEG), F32),
            pltpu.VMEM((4, 4, 1, 128), F32),
            pltpu.VMEM((4, 4, 1, 128), F32),
            pltpu.VMEM(head4, F32),
        ],
        flops=4 * 6 * 2 * 512 * 1024 * 128,
        name="main",
    )
    back2, back1, back3 = shift(send2, "z", 2), shift(send1, "z", 1), shift(send3, "z", -1)
    att_pieces = y_return(att)
    wide = S((4, DH, SEG), F32)
    dk, dv, q_adj, q_raw, q_s = call(
        level_backward_kernel,
        (ids, q, g, k0, v0, lse, delta, dq, dk, dv, *qg_pieces, q_gain),
        1,
        (S(head4, F32), S(head4, F32), wide, wide, row),
        [pltpu.VMEM(head4, F32)],
        flops=7 * 5 * 2 * 512 * 512 * 128,
        name="level_backward",
    )
    q_inner = to_all(q_s.reshape(4, SEG))
    dq_slots = call(
        final_q_kernel, (ids, q_inner, stats, q_adj, q_raw), 1, S((4, SEG, DH), BF16), name="final_q"
    )
    dq_pieces = y_return(dq_slots)
    dv_slots, k_adj, k_raw, k_s = call(
        collect_kernel,
        (ids, dk, dv, back1, back2, back3, *kv_pieces, k_gain),
        1,
        (S((4, SEG, DH), BF16), wide, wide, row),
        name="collect",
    )
    k_inner = to_all(k_s.reshape(4, SEG))
    dv_pieces = y_return(dv_slots)
    dk_slots = call(
        final_k_kernel, (ids, k_inner, stats, k_adj, k_raw), 1, S((4, SEG, DH), BF16), name="final_k"
    )
    dk_pieces = y_return(dk_slots)
    flat = S((SEG, 4 * DH), BF16)
    attended, query_grads, value_grads = call(
        restore_kernel,
        (ids, *att_pieces, *dq_pieces, *dv_pieces),
        1,
        (flat, flat, flat),
        name="restore",
    )
    (key_grads,) = call(restore_kernel, (ids, *dk_pieces), 1, (flat,), name="restore_k")
    return (attended, query_grads, key_grads, value_grads)


def solution(mesh):
    split = Mesh(mesh.devices.reshape(4, 4, 8), ("z", "y", "head"))
    big = P(("z", "y"), "head")
    in_specs = (big, big, big, P("head"), P("head"), P(), big)
    return jax.shard_map(
        shards, mesh=split, in_specs=in_specs, out_specs=(big, big, big, big), check_vma=False
    )
```

profile of v0, /device:TPU:0, one launch (start us, length us, event | category | flops | bytes accessed | tf_op | source)
XLA Modules:
  0.0 194.6 jit_solution(8132171774206715991)
XLA Ops:
  1.3 5.6 %prep.1 = (bf16[4,2,512,128]{3,2,1,0:T(8,128)(2,1)}, bf16[4,2,512,128]{3,2,1,0:T(8,128)(2,1)}, f32[8,512]{1,0:T(8,128)}) custom-call(s32[3]{0:T(128)} %pad_add_fusion.ids, bf16[512,512]{1,0:T(8,128)(2,1)} %q.1, bf16[512,512]{1,0:T(8,128)(2,1)} %k.1, bf16[512,512]{1,0:T(8,128)(2,1)} %v.1, bf16[512,512]{1,0:T(8,128)(2,1)} %g.1), custom_call_target="tpu_custom_call" | custom-call | flops 1073741824 | bytes 4194304 | tf_op jit(solution)/shard_map/prep/pallas_call | solution.py:50
  8.9 3.1 %collective-permute-start.5 = (bf16[2,512,128]{2,1,0:T(8,128)(2,1)S(1)}, bf16[2,512,128]{2,1,0:T(8,128)(2,1)S(1)}, u32[]{:S(2)}, u32[]{:S(2)}) collective-permute-start(bf16[2,512,128]{2,1,0:T(8,128)(2,1)S(1)} %get-tuple-element.62), channel_id=1, source_target_pairs={{0,24},{8,0},{16,8},{24,16},{1,25},{9,1},{17,9},{25,17},{2,26},{10... | collective-permute-start | bytes 786440 | tf_op jit(solution)/shard_map/ppermute | solution.py:458
  15.0 6.4 %all-to-all-start = ((f32[32,2,512]{2,1,0:T(2,128)}), f32[32,2,512]{2,1,0:T(2,128)S(1)}, u32[]{:S(2)}, u32[]{:S(2)}) async-start(f32[32,2,512]{2,1,0:T(2,128)} %broadcast_in_dim.11), calls=%async_computation | async-start | bytes 262144 | tf_op jit(solution)/shard_map/all_to_all | solution.py:471
  22.8 6.4 %all-to-all-done.stats = f32[32,2,512]{2,1,0:T(2,128)S(1)} async-done(((f32[32,2,512]{2,1,0:T(2,128)}), f32[32,2,512]{2,1,0:T(2,128)S(1)}, u32[]{:S(2)}, u32[]{:S(2)}) %all-to-all-start) | async-done | bytes 131104 | tf_op jit(solution)/shard_map/all_to_all | solution.py:471
  30.1 2.7 %norm_k.1.k.k0 = bf16[4,4,128,128]{3,2,1,0:T(8,128)(2,1)} custom-call(s32[3]{0:T(128)} %pad_add_fusion.ids, bf16[2,512,128]{2,1,0:T(8,128)(2,1)} %get-tuple-element.65.p0, bf16[2,512,128]{2,1,0:T(8,128)(2,1)} %copy-done.3, bf16[2,512,128]{2,1,0:T(8,128)(2,1)} %copy-done.2, bf16[2,512,128]{2,1,0:T(8,128)(2,1)} %copy-done.1, f32[32,2,512]{2,1,0:T(2,128)} %copy-done, ...), custom_call_target="tpu_custom_call" | custom-call | bytes 4194304 | tf_op jit(solution)/shard_map/norm_k/pallas_call | solution.py:50
  34.7 2.0 %place_v.1.v.v0 = bf16[4,4,128,128]{3,2,1,0:T(8,128)(2,1)} custom-call(s32[3]{0:T(128)} %pad_add_fusion.ids, bf16[2,512,128]{2,1,0:T(8,128)(2,1)} %get-tuple-element.65.p0, bf16[2,512,128]{2,1,0:T(8,128)(2,1)} %copy-done.3, bf16[2,512,128]{2,1,0:T(8,128)(2,1)} %copy-done.2, bf16[2,512,128]{2,1,0:T(8,128)(2,1)} %copy-done.1), custom_call_target="tpu_custom_call" | custom-call | bytes 4194304 | tf_op jit(solution)/shard_map/place_v/pallas_call | solution.py:50
  36.8 2.2 %collective-permute-start.7 = (bf16[4,4,128,128]{3,2,1,0:T(8,128)(2,1)}, bf16[4,4,128,128]{3,2,1,0:T(8,128)(2,1)}, u32[]{:S(2)}, u32[]{:S(2)}) collective-permute-start(bf16[4,4,128,128]{3,2,1,0:T(8,128)(2,1)} %place_v.1.v.v0), channel_id=1, source_target_pairs={{0,96},{32,0},{64,32},{96,64},{1,97},{33,1},{65,33},{97,65},{2,98}... | collective-permute-start | bytes 1572872 | tf_op jit(solution)/shard_map/ppermute | solution.py:458
  44.4 4.6 %collective-permute-done.2.p3 = bf16[2,512,128]{2,1,0:T(8,128)(2,1)S(1)} collective-permute-done((bf16[2,512,128]{2,1,0:T(8,128)(2,1)S(1)}, bf16[2,512,128]{2,1,0:T(8,128)(2,1)S(1)}, u32[]{:S(2)}, u32[]{:S(2)}) %collective-permute-start.2) | collective-permute-done | bytes 262176 | tf_op jit(solution)/shard_map/ppermute | solution.py:458
  51.9 3.4 %collective-permute-start.10 = (bf16[4,4,128,128]{3,2,1,0:T(8,128)(2,1)}, bf16[4,4,128,128]{3,2,1,0:T(8,128)(2,1)}, u32[]{:S(2)}, u32[]{:S(2)}) collective-permute-start(bf16[4,4,128,128]{3,2,1,0:T(8,128)(2,1)} %collective-permute-done.7.v1), channel_id=1, source_target_pairs={{0,96},{32,0},{64,32},{96,64},{1,97},{33,1},{65,33},{97,65},{2,98}... | collective-permute-start | bytes 1572872 | tf_op jit(solution)/shard_map/ppermute | solution.py:458
  58.0 4.9 %collective-permute-done.p1 = bf16[2,512,128]{2,1,0:T(8,128)(2,1)S(1)} collective-permute-done((bf16[2,512,128]{2,1,0:T(8,128)(2,1)S(1)}, bf16[2,512,128]{2,1,0:T(8,128)(2,1)S(1)}, u32[]{:S(2)}, u32[]{:S(2)}) %collective-permute-start) | collective-permute-done | bytes 262176 | tf_op jit(solution)/shard_map/ppermute | solution.py:458
  63.6 2.8 %norm_q.1 = (bf16[4,4,128,128]{3,2,1,0:T(8,128)(2,1)}, bf16[4,4,128,128]{3,2,1,0:T(8,128)(2,1)}) custom-call(s32[3]{0:T(128)} %pad_add_fusion.ids, bf16[2,512,128]{2,1,0:T(8,128)(2,1)} %get-tuple-element.69.p0, bf16[2,512,128]{2,1,0:T(8,128)(2,1)} %copy-done.16, bf16[2,512,128]{2,1,0:T(8,128)(2,1)} %copy-done.15, bf16[2,512,128]{2,1,0:T(8,128)(2,1)} %copy-done.14, ...), custom_call_target="tpu_custom_call" | custom-call | bytes 4194304 | tf_op jit(solution)/shard_map/norm_q/pallas_call | solution.py:50
  66.4 7.8 %level_forward.1 = (f32[4,4,1,128]{3,2,1,0:T(1,128)}, f32[4,4,1,128]{3,2,1,0:T(1,128)}, f32[4,4,128,128]{3,2,1,0:T(8,128)}) custom-call(s32[3]{0:T(128)} %pad_add_fusion.ids, bf16[4,4,128,128]{3,2,1,0:T(8,128)(2,1)} %get-tuple-element.35.q, bf16[4,4,128,128]{3,2,1,0:T(8,128)(2,1)} %norm_k.1.k.k0, bf16[4,4,128,128]{3,2,1,0:T(8,128)(2,1)} %place_v.1.v.v0), custom_call_target="tpu_custom_call" | custom-call | flops 939524096 | bytes 4194304 | tf_op jit(solution)/shard_map/level_forward/pallas_call | solution.py:50
  74.2 22.8 %main.1 = (bf16[4,512,128]{2,1,0:T(8,128)(2,1)}, f32[4,4,128,128]{3,2,1,0:T(8,128)}, f32[4,1,512]{2,1,0:T(1,128)}, f32[4,1,512]{2,1,0:T(1,128)}, bf16[2,4,4,128,...) custom-call(s32[3]{0:T(128)} %pad_add_fusion.ids, ...), custom_call_target="tpu_custom_call" | custom-call | flops 3221225472 | bytes 4194304 | tf_op jit(solution)/shard_map/main/pallas_call | solution.py:50
  97.9 3.2 %collective-permute-start.19 = (bf16[2,4,4,128,128]{4,3,2,1,0:T(8,128)(2,1)}, bf16[2,4,4,128,128]{4,3,2,1,0:T(8,128)(2,1)S(1)}, u32[]{:S(2)}, u32[]{:S(2)}) collective-permute-start(bf16[2,4,4,128,128]{4,3,2,1,0:T(8,128)(2,1)} %get-tuple-element.53), channel_id=1, source_target_pairs={{0,64},{32,96},{64,0},{96,32},{1,65},{33,97},{65,1},{97,33},{2,66}... | collective-permute-start | bytes 3145736 | tf_op jit(solution)/shard_map/ppermute | solution.py:458
  102.2 14.5 %level_backward.1 = (f32[4,4,128,128]{3,2,1,0:T(8,128)}, f32[4,4,128,128]{3,2,1,0:T(8,128)}, f32[4,128,512]{2,1,0:T(8,128)}, f32[4,128,512]{2,1,0:T(8,128)}, f32[4,1,512]{2,1,0:T(1,128)}) custom-call(s32[3]{0:T(128)} %pad_add_fusion.ids, bf16[4,4,128,128]{3,2,1,0:T(8,128)(2,1)} %get-tuple-element.35.q, bf16[4,4,128,128]{3,2,1,0:T(8,128)(2,1)} %get-tuple-element.36.g, ...), custom_call_target="tpu_custom_call" | custom-call | flops 2348810240 | bytes 4194304 | tf_op jit(solution)/shard_map/level_backward/pallas_call | solution.py:50
  118.1 3.9 %all-to-all-start.1 = ((f32[32,4,512]{2,1,0:T(4,128)}), f32[32,4,512]{2,1,0:T(4,128)S(1)}, u32[]{:S(2)}, u32[]{:S(2)}) async-start(f32[32,4,512]{2,1,0:T(4,128)} %broadcast_in_dim.12), calls=%async_computation.1 | async-start | bytes 524288 | tf_op jit(solution)/shard_map/all_to_all | solution.py:471
  123.9 3.0 %collective-permute-start.14 = (bf16[512,128]{1,0:T(8,128)(2,1)}, bf16[512,128]{1,0:T(8,128)(2,1)S(1)}, u32[]{:S(2)}, u32[]{:S(2)}) collective-permute-start(bf16[512,128]{1,0:T(8,128)(2,1)} %get-tuple-element.82), channel_id=1, source_target_pairs={{0,24},{8,0},{16,8},{24,16},{1,25},{9,1},{17,9},{25,17},{2,26},{10... | collective-permute-start | bytes 393224 | tf_op jit(solution)/shard_map/ppermute | solution.py:458
  127.7 3.1 %all-to-all-done.1.inner = f32[32,4,512]{2,1,0:T(4,128)S(1)} async-done(((f32[32,4,512]{2,1,0:T(4,128)}), f32[32,4,512]{2,1,0:T(4,128)S(1)}, u32[]{:S(2)}, u32[]{:S(2)}) %all-to-all-start.1) | async-done | bytes 262176 | tf_op jit(solution)/shard_map/all_to_all | solution.py:471
  131.5 2.9 %final_q.1 = bf16[4,512,128]{2,1,0:T(8,128)(2,1)} custom-call(s32[3]{0:T(128)} %pad_add_fusion.ids, f32[32,4,512]{2,1,0:T(4,128)} %copy-done.9, f32[32,2,512]{2,1,0:T(2,128)} %copy-done, f32[4,128,512]{2,1,0:T(8,128)} %get-tuple-element.48.adj, f32[4,128,512]{2,1,0:T(8,128)} %get-tuple-element.49.raw), custom_call_target="tpu_custom_call" | custom-call | bytes 4194304 | tf_op jit(solution)/shard_map/final_q/pallas_call | solution.py:50
  134.8 11.2 %collective-permute-done.19.r2 = bf16[2,4,4,128,128]{4,3,2,1,0:T(8,128)(2,1)S(1)} collective-permute-done((bf16[2,4,4,128,128]{4,3,2,1,0:T(8,128)(2,1)}, bf16[2,4,4,128,128]{4,3,2,1,0:T(8,128)(2,1)S(1)}, u32[]{:S(2)}, u32[]{:S(2)}) %collective-permute-start.19) | collective-permute-done | bytes 1048608 | tf_op jit(solution)/shard_map/ppermute | solution.py:458
  147.4 4.9 %collect.1 = (bf16[4,512,128]{2,1,0:T(8,128)(2,1)}, f32[4,128,512]{2,1,0:T(8,128)}, f32[4,128,512]{2,1,0:T(8,128)}, f32[4,1,512]{2,1,0:T(1,128)}) custom-call(s32[3]{0:T(128)} %pad_add_fusion.ids, f32[4,4,128,128]{3,2,1,0:T(8,128)} %get-tuple-element.50.dk, f32[4,4,128,128]{3,2,1,0:T(8,128)} %get-tuple-element.51.dv, bf16[2,4,4,128,128]{4,3,2,1,0:T(8,128)(2,1)} %copy-done.5, ...), custom_call_target="tpu_custom_call" | custom-call | bytes 4194304 | tf_op jit(solution)/shard_map/collect/pallas_call | solution.py:50
  153.8 3.9 %all-to-all-start.2 = ((f32[32,4,512]{2,1,0:T(4,128)}), f32[32,4,512]{2,1,0:T(4,128)S(1)}, u32[]{:S(2)}, u32[]{:S(2)}) async-start(f32[32,4,512]{2,1,0:T(4,128)} %broadcast_in_dim.13), calls=%async_computation.2 | async-start | bytes 524288 | tf_op jit(solution)/shard_map/all_to_all | solution.py:471
  158.4 3.0 %collective-permute-start.17 = (bf16[512,128]{1,0:T(8,128)(2,1)S(1)}, bf16[512,128]{1,0:T(8,128)(2,1)S(1)}, u32[]{:S(2)}, u32[]{:S(2)}) collective-permute-start(bf16[512,128]{1,0:T(8,128)(2,1)S(1)} %get-tuple-element.78), channel_id=1, source_target_pairs={{0,24},{8,0},{16,8},{24,16},{1,25},{9,1},{17,9},{25,17},{2,26},{10... | collective-permute-start | bytes 393224 | tf_op jit(solution)/shard_map/ppermute | solution.py:458
  162.9 3.8 %all-to-all-done.2.inner = f32[32,4,512]{2,1,0:T(4,128)S(1)} async-done(((f32[32,4,512]{2,1,0:T(4,128)}), f32[32,4,512]{2,1,0:T(4,128)S(1)}, u32[]{:S(2)}, u32[]{:S(2)}) %all-to-all-start.2) | async-done | bytes 262176 | tf_op jit(solution)/shard_map/all_to_all | solution.py:471
  167.3 2.9 %final_k.1 = bf16[4,512,128]{2,1,0:T(8,128)(2,1)} custom-call(s32[3]{0:T(128)} %pad_add_fusion.ids, f32[32,4,512]{2,1,0:T(4,128)} %copy-done.8, f32[32,2,512]{2,1,0:T(2,128)} %copy-done, f32[4,128,512]{2,1,0:T(8,128)} %get-tuple-element.59.adj, f32[4,128,512]{2,1,0:T(8,128)} %get-tuple-element.60.raw), custom_call_target="tpu_custom_call" | custom-call | bytes 4194304 | tf_op jit(solution)/shard_map/final_k/pallas_call | solution.py:50
  170.5 2.9 %collective-permute-start.23 = (bf16[512,128]{1,0:T(8,128)(2,1)S(1)}, bf16[512,128]{1,0:T(8,128)(2,1)S(1)}, u32[]{:S(2)}, u32[]{:S(2)}) collective-permute-start(bf16[512,128]{1,0:T(8,128)(2,1)S(1)} %get-tuple-element.74), channel_id=1, source_target_pairs={{0,24},{8,0},{16,8},{24,16},{1,25},{9,1},{17,9},{25,17},{2,26},{10... | collective-permute-start | bytes 393224 | tf_op jit(solution)/shard_map/ppermute | solution.py:458
  176.2 2.5 %collective-permute-start.26 = (bf16[512,128]{1,0:T(8,128)(2,1)S(1)}, bf16[512,128]{1,0:T(8,128)(2,1)S(1)}, u32[]{:S(2)}, u32[]{:S(2)}) collective-permute-start(bf16[512,128]{1,0:T(8,128)(2,1)S(1)} %get-tuple-element.70), channel_id=1, source_target_pairs={{0,24},{8,0},{16,8},{24,16},{1,25},{9,1},{17,9},{25,17},{2,26},{10... | collective-permute-start | bytes 393224 | tf_op jit(solution)/shard_map/ppermute | solution.py:458
  178.7 2.2 %collective-permute-start.25 = (bf16[512,128]{1,0:T(8,128)(2,1)S(1)}, bf16[512,128]{1,0:T(8,128)(2,1)S(1)}, u32[]{:S(2)}, u32[]{:S(2)}) collective-permute-start(bf16[512,128]{1,0:T(8,128)(2,1)S(1)} %get-tuple-element.71), channel_id=1, source_target_pairs={{0,16},{8,24},{16,0},{24,8},{1,17},{9,25},{17,1},{25,9},{2,18},{10... | collective-permute-start | bytes 393224 | tf_op jit(solution)/shard_map/ppermute | solution.py:458
  180.9 2.3 %collective-permute-done.22.refs_10_ = bf16[512,128]{1,0:T(8,128)(2,1)S(1)} collective-permute-done((bf16[512,128]{1,0:T(8,128)(2,1)S(1)}, bf16[512,128]{1,0:T(8,128)(2,1)S(1)}, u32[]{:S(2)}, u32[]{:S(2)}) %collective-permute-start.22) | collective-permute-done | bytes 131104 | tf_op jit(solution)/shard_map/ppermute | solution.py:458
  183.2 3.2 %collective-permute-done.21.refs_9_ = bf16[512,128]{1,0:T(8,128)(2,1)S(1)} collective-permute-done((bf16[512,128]{1,0:T(8,128)(2,1)S(1)}, bf16[512,128]{1,0:T(8,128)(2,1)S(1)}, u32[]{:S(2)}, u32[]{:S(2)}) %collective-permute-start.21) | collective-permute-done | bytes 131104 | tf_op jit(solution)/shard_map/ppermute | solution.py:458
  187.0 4.2 %restore.1 = (bf16[512,512]{1,0:T(8,128)(2,1)}, bf16[512,512]{1,0:T(8,128)(2,1)}, bf16[512,512]{1,0:T(8,128)(2,1)}) custom-call(s32[3]{0:T(128)} %pad_add_fusion.ids, bf16[512,128]{1,0:T(8,128)(2,1)} %get-tuple-element.85.refs_0_, bf16[512,128]{1,0:T(8,128)(2,1)} %copy-done.18, bf16[512,128]{1,0:T(8,128)(2,1)} %collective-permute-done.13.refs_2_, ...), custom_call_target="tpu_custom_call" | custom-call | bytes 4194304 | tf_op jit(solution)/shard_map/restore/pallas_call | solution.py:50
  192.0 2.6 %restore_k.1 = bf16[512,512]{1,0:T(8,128)(2,1)} custom-call(s32[3]{0:T(128)} %pad_add_fusion.ids, bf16[512,128]{1,0:T(8,128)(2,1)} %get-tuple-element.73.refs_0_, bf16[512,128]{1,0:T(8,128)(2,1)} %copy-done.27, bf16[512,128]{1,0:T(8,128)(2,1)} %copy-done.26, bf16[512,128]{1,0:T(8,128)(2,1)} %copy-done.25), custom_call_target="tpu_custom_call" | custom-call | bytes 4194304 | tf_op jit(solution)/shard_map/restore_k/pallas_call | solution.py:50
  (122 shorter events, 38.8 us)
Async XLA Ops:
  8.9 20.3 %collective-permute-start.5 = (bf16[2,512,128]{2,1,0:T(8,128)(2,1)S(1)}, bf16[2,512,128]{2,1,0:T(8,128)(2,1)S(1)}, u32[]{:S(2)}, u32[]{:S(2)}) collective-permute-start(bf16[2,512,128]{2,1,0:T(8,128)(2,1)S(1)} %get-tuple-element.62), channel_id=1, source_target_pairs={{0,24},{8,0},{16,8},{24,16},{1,25},{9,1},{17,9},{25,17},{2,26},{10... | collective-permute-start | bytes 786440 | tf_op jit(solution)/shard_map/ppermute | solution.py:458
  12.0 17.2 %collective-permute-start.4 = (bf16[2,512,128]{2,1,0:T(8,128)(2,1)S(1)}, bf16[2,512,128]{2,1,0:T(8,128)(2,1)S(1)}, u32[]{:S(2)}, u32[]{:S(2)}) collective-permute-start(bf16[2,512,128]{2,1,0:T(8,128)(2,1)S(1)} %get-tuple-element.63), channel_id=1, source_target_pairs={{0,16},{8,24},{16,0},{24,8},{1,17},{9,25},{17,1},{25,9},{2,18},{10... | collective-permute-start | bytes 786440 | tf_op jit(solution)/shard_map/ppermute | solution.py:458
  12.6 16.6 %collective-permute-start.3 = (bf16[2,512,128]{2,1,0:T(8,128)(2,1)S(1)}, bf16[2,512,128]{2,1,0:T(8,128)(2,1)S(1)}, u32[]{:S(2)}, u32[]{:S(2)}) collective-permute-start(bf16[2,512,128]{2,1,0:T(8,128)(2,1)S(1)} %get-tuple-element.64), channel_id=1, source_target_pairs={{0,8},{8,16},{16,24},{24,0},{1,9},{9,17},{17,25},{25,1},{2,10},{10... | collective-permute-start | bytes 786440 | tf_op jit(solution)/shard_map/ppermute | solution.py:458
  15.0 14.2 %all-to-all-start = ((f32[32,2,512]{2,1,0:T(2,128)}), f32[32,2,512]{2,1,0:T(2,128)S(1)}, u32[]{:S(2)}, u32[]{:S(2)}) async-start(f32[32,2,512]{2,1,0:T(2,128)} %broadcast_in_dim.11), calls=%async_computation | async-start | bytes 262144 | tf_op jit(solution)/shard_map/all_to_all | solution.py:471
  32.8 16.4 %collective-permute-start.8 = (bf16[4,4,128,128]{3,2,1,0:T(8,128)(2,1)}, bf16[4,4,128,128]{3,2,1,0:T(8,128)(2,1)S(1)}, u32[]{:S(2)}, u32[]{:S(2)}) collective-permute-start(bf16[4,4,128,128]{3,2,1,0:T(8,128)(2,1)} %norm_k.1.k.k0), channel_id=1, source_target_pairs={{0,32},{32,64},{64,96},{96,0},{1,33},{33,65},{65,97},{97,1},{2,34}... | collective-permute-start | bytes 1572872 | tf_op jit(solution)/shard_map/ppermute | solution.py:458
  36.8 15.1 %collective-permute-start.7 = (bf16[4,4,128,128]{3,2,1,0:T(8,128)(2,1)}, bf16[4,4,128,128]{3,2,1,0:T(8,128)(2,1)}, u32[]{:S(2)}, u32[]{:S(2)}) collective-permute-start(bf16[4,4,128,128]{3,2,1,0:T(8,128)(2,1)} %place_v.1.v.v0), channel_id=1, source_target_pairs={{0,96},{32,0},{64,32},{96,64},{1,97},{33,1},{65,33},{97,65},{2,98}... | collective-permute-start | bytes 1572872 | tf_op jit(solution)/shard_map/ppermute | solution.py:458
  39.8 16.1 %copy-start.28 = (s32[16,8]{0,1:T(8,128)S(1)}, s32[16,8]{0,1:T(8,128)}, u32[]{:S(2)}) copy-start(s32[16,8]{0,1:T(8,128)} %param.12) | copy-start | bytes 1540
  39.8 9.2 %collective-permute-start.2 = (bf16[2,512,128]{2,1,0:T(8,128)(2,1)S(1)}, bf16[2,512,128]{2,1,0:T(8,128)(2,1)S(1)}, u32[]{:S(2)}, u32[]{:S(2)}) collective-permute-start(bf16[2,512,128]{2,1,0:T(8,128)(2,1)S(1)} %get-tuple-element.66), channel_id=1, source_target_pairs={{0,24},{8,0},{16,8},{24,16},{1,25},{9,1},{17,9},{25,17},{2,26},{10... | collective-permute-start | bytes 786440 | tf_op jit(solution)/shard_map/ppermute | solution.py:458
  40.9 14.4 %collective-permute-start.1 = (bf16[2,512,128]{2,1,0:T(8,128)(2,1)S(1)}, bf16[2,512,128]{2,1,0:T(8,128)(2,1)S(1)}, u32[]{:S(2)}, u32[]{:S(2)}) collective-permute-start(bf16[2,512,128]{2,1,0:T(8,128)(2,1)S(1)} %get-tuple-element.67), channel_id=1, source_target_pairs={{0,16},{8,24},{16,0},{24,8},{1,17},{9,25},{17,1},{25,9},{2,18},{10... | collective-permute-start | bytes 786440 | tf_op jit(solution)/shard_map/ppermute | solution.py:458
  42.4 31.8 %collective-permute-start.6 = (bf16[4,4,128,128]{3,2,1,0:T(8,128)(2,1)S(1)}, bf16[4,4,128,128]{3,2,1,0:T(8,128)(2,1)}, u32[]{:S(2)}, u32[]{:S(2)}) collective-permute-start(bf16[4,4,128,128]{3,2,1,0:T(8,128)(2,1)S(1)} %copy-done.13), channel_id=1, source_target_pairs={{0,96},{32,0},{64,32},{96,64},{1,97},{33,1},{65,33},{97,65},{2,98}... | collective-permute-start | bytes 1572872 | tf_op jit(solution)/shard_map/ppermute | solution.py:458
  48.9 25.3 %collective-permute-start.11 = (bf16[4,4,128,128]{3,2,1,0:T(8,128)(2,1)S(1)}, bf16[4,4,128,128]{3,2,1,0:T(8,128)(2,1)}, u32[]{:S(2)}, u32[]{:S(2)}) collective-permute-start(bf16[4,4,128,128]{3,2,1,0:T(8,128)(2,1)S(1)} %copy-done.11), channel_id=1, source_target_pairs={{0,32},{32,64},{64,96},{96,0},{1,33},{33,65},{65,97},{97,1},{2,34}... | collective-permute-start | bytes 1572872 | tf_op jit(solution)/shard_map/ppermute | solution.py:458
  49.2 25.0 %copy-start.29 = (bf16[4,4,128,128]{3,2,1,0:T(8,128)(2,1)}, bf16[4,4,128,128]{3,2,1,0:T(8,128)(2,1)S(1)}, u32[]{:S(2)}) copy-start(bf16[4,4,128,128]{3,2,1,0:T(8,128)(2,1)S(1)} %collective-permute-done.8.k3) | copy-start | bytes 1572868
  49.3 25.0 %collective-permute-start.9 = (bf16[4,4,128,128]{3,2,1,0:T(8,128)(2,1)S(1)}, bf16[4,4,128,128]{3,2,1,0:T(8,128)(2,1)}, u32[]{:S(2)}, u32[]{:S(2)}) collective-permute-start(bf16[4,4,128,128]{3,2,1,0:T(8,128)(2,1)S(1)} %collective-permute-done.8.k3), channel_id=1, source_target_pairs={{0,32},{32,64},{64,96},{96,0},{1,33},{33,65},{65,97},{97,1},{2,34}... | collective-permute-start | bytes 1572872 | tf_op jit(solution)/shard_map/ppermute | solution.py:458
  51.9 22.4 %collective-permute-start.10 = (bf16[4,4,128,128]{3,2,1,0:T(8,128)(2,1)}, bf16[4,4,128,128]{3,2,1,0:T(8,128)(2,1)}, u32[]{:S(2)}, u32[]{:S(2)}) collective-permute-start(bf16[4,4,128,128]{3,2,1,0:T(8,128)(2,1)} %collective-permute-done.7.v1), channel_id=1, source_target_pairs={{0,96},{32,0},{64,32},{96,64},{1,97},{33,1},{65,33},{97,65},{2,98}... | collective-permute-start | bytes 1572872 | tf_op jit(solution)/shard_map/ppermute | solution.py:458
  55.3 7.6 %collective-permute-start = (bf16[2,512,128]{2,1,0:T(8,128)(2,1)S(1)}, bf16[2,512,128]{2,1,0:T(8,128)(2,1)S(1)}, u32[]{:S(2)}, u32[]{:S(2)}) collective-permute-start(bf16[2,512,128]{2,1,0:T(8,128)(2,1)S(1)} %get-tuple-element.68), channel_id=1, source_target_pairs={{0,8},{8,16},{16,24},{24,0},{1,9},{9,17},{17,25},{25,1},{2,10},{10... | collective-permute-start | bytes 786440 | tf_op jit(solution)/shard_map/ppermute | solution.py:458
  97.0 37.4 %collective-permute-start.18 = (bf16[2,4,4,128,128]{4,3,2,1,0:T(8,128)(2,1)}, bf16[2,4,4,128,128]{4,3,2,1,0:T(8,128)(2,1)S(1)}, u32[]{:S(2)}, u32[]{:S(2)}) collective-permute-start(bf16[2,4,4,128,128]{4,3,2,1,0:T(8,128)(2,1)} %get-tuple-element.52), channel_id=1, source_target_pairs={{0,32},{32,64},{64,96},{96,0},{1,33},{33,65},{65,97},{97,1},{2,34}... | collective-permute-start | bytes 3145736 | tf_op jit(solution)/shard_map/ppermute | solution.py:458
  97.9 48.2 %collective-permute-start.19 = (bf16[2,4,4,128,128]{4,3,2,1,0:T(8,128)(2,1)}, bf16[2,4,4,128,128]{4,3,2,1,0:T(8,128)(2,1)S(1)}, u32[]{:S(2)}, u32[]{:S(2)}) collective-permute-start(bf16[2,4,4,128,128]{4,3,2,1,0:T(8,128)(2,1)} %get-tuple-element.53), channel_id=1, source_target_pairs={{0,64},{32,96},{64,0},{96,32},{1,65},{33,97},{65,1},{97,33},{2,66}... | collective-permute-start | bytes 3145736 | tf_op jit(solution)/shard_map/ppermute | solution.py:458
  101.1 45.0 %collective-permute-start.20 = (bf16[2,4,4,128,128]{4,3,2,1,0:T(8,128)(2,1)}, bf16[2,4,4,128,128]{4,3,2,1,0:T(8,128)(2,1)S(1)}, u32[]{:S(2)}, u32[]{:S(2)}) collective-permute-start(bf16[2,4,4,128,128]{4,3,2,1,0:T(8,128)(2,1)} %get-tuple-element.54), channel_id=1, source_target_pairs={{0,96},{32,0},{64,32},{96,64},{1,97},{33,1},{65,33},{97,65},{2,98}... | collective-permute-start | bytes 3145736 | tf_op jit(solution)/shard_map/ppermute | solution.py:458
  118.1 12.7 %all-to-all-start.1 = ((f32[32,4,512]{2,1,0:T(4,128)}), f32[32,4,512]{2,1,0:T(4,128)S(1)}, u32[]{:S(2)}, u32[]{:S(2)}) async-start(f32[32,4,512]{2,1,0:T(4,128)} %broadcast_in_dim.12), calls=%async_computation.1 | async-start | bytes 524288 | tf_op jit(solution)/shard_map/all_to_all | solution.py:471
  123.9 46.3 %collective-permute-start.14 = (bf16[512,128]{1,0:T(8,128)(2,1)}, bf16[512,128]{1,0:T(8,128)(2,1)S(1)}, u32[]{:S(2)}, u32[]{:S(2)}) collective-permute-start(bf16[512,128]{1,0:T(8,128)(2,1)} %get-tuple-element.82), channel_id=1, source_target_pairs={{0,24},{8,0},{16,8},{24,16},{1,25},{9,1},{17,9},{25,17},{2,26},{10... | collective-permute-start | bytes 393224 | tf_op jit(solution)/shard_map/ppermute | solution.py:458
  127.0 43.5 %collective-permute-start.13 = (bf16[512,128]{1,0:T(8,128)(2,1)}, bf16[512,128]{1,0:T(8,128)(2,1)}, u32[]{:S(2)}, u32[]{:S(2)}) collective-permute-start(bf16[512,128]{1,0:T(8,128)(2,1)} %get-tuple-element.83), channel_id=1, source_target_pairs={{0,16},{8,24},{16,0},{24,8},{1,17},{9,25},{17,1},{25,9},{2,18},{10... | collective-permute-start | bytes 393224 | tf_op jit(solution)/shard_map/ppermute | solution.py:458
  134.4 40.8 %collective-permute-start.12 = (bf16[512,128]{1,0:T(8,128)(2,1)}, bf16[512,128]{1,0:T(8,128)(2,1)S(1)}, u32[]{:S(2)}, u32[]{:S(2)}) collective-permute-start(bf16[512,128]{1,0:T(8,128)(2,1)} %get-tuple-element.84), channel_id=1, source_target_pairs={{0,8},{8,16},{16,24},{24,0},{1,9},{9,17},{17,25},{25,1},{2,10},{10... | collective-permute-start | bytes 393224 | tf_op jit(solution)/shard_map/ppermute | solution.py:458
  153.8 12.8 %all-to-all-start.2 = ((f32[32,4,512]{2,1,0:T(4,128)}), f32[32,4,512]{2,1,0:T(4,128)S(1)}, u32[]{:S(2)}, u32[]{:S(2)}) async-start(f32[32,4,512]{2,1,0:T(4,128)} %broadcast_in_dim.13), calls=%async_computation.2 | async-start | bytes 524288 | tf_op jit(solution)/shard_map/all_to_all | solution.py:471
  158.4 16.9 %collective-permute-start.17 = (bf16[512,128]{1,0:T(8,128)(2,1)S(1)}, bf16[512,128]{1,0:T(8,128)(2,1)S(1)}, u32[]{:S(2)}, u32[]{:S(2)}) collective-permute-start(bf16[512,128]{1,0:T(8,128)(2,1)S(1)} %get-tuple-element.78), channel_id=1, source_target_pairs={{0,24},{8,0},{16,8},{24,16},{1,25},{9,1},{17,9},{25,17},{2,26},{10... | collective-permute-start | bytes 393224 | tf_op jit(solution)/shard_map/ppermute | solution.py:458
  161.4 14.7 %collective-permute-start.16 = (bf16[512,128]{1,0:T(8,128)(2,1)S(1)}, bf16[512,128]{1,0:T(8,128)(2,1)S(1)}, u32[]{:S(2)}, u32[]{:S(2)}) collective-permute-start(bf16[512,128]{1,0:T(8,128)(2,1)S(1)} %get-tuple-element.79), channel_id=1, source_target_pairs={{0,16},{8,24},{16,0},{24,8},{1,17},{9,25},{17,1},{25,9},{2,18},{10... | collective-permute-start | bytes 393224 | tf_op jit(solution)/shard_map/ppermute | solution.py:458
  170.2 8.5 %collective-permute-start.15 = (bf16[512,128]{1,0:T(8,128)(2,1)S(1)}, bf16[512,128]{1,0:T(8,128)(2,1)S(1)}, u32[]{:S(2)}, u32[]{:S(2)}) collective-permute-start(bf16[512,128]{1,0:T(8,128)(2,1)S(1)} %get-tuple-element.80), channel_id=1, source_target_pairs={{0,8},{8,16},{16,24},{24,0},{1,9},{9,17},{17,25},{25,1},{2,10},{10... | collective-permute-start | bytes 393224 | tf_op jit(solution)/shard_map/ppermute | solution.py:458
  170.5 10.4 %collective-permute-start.23 = (bf16[512,128]{1,0:T(8,128)(2,1)S(1)}, bf16[512,128]{1,0:T(8,128)(2,1)S(1)}, u32[]{:S(2)}, u32[]{:S(2)}) collective-permute-start(bf16[512,128]{1,0:T(8,128)(2,1)S(1)} %get-tuple-element.74), channel_id=1, source_target_pairs={{0,24},{8,0},{16,8},{24,16},{1,25},{9,1},{17,9},{25,17},{2,26},{10... | collective-permute-start | bytes 393224 | tf_op jit(solution)/shard_map/ppermute | solution.py:458
  175.2 8.0 %collective-permute-start.22 = (bf16[512,128]{1,0:T(8,128)(2,1)S(1)}, bf16[512,128]{1,0:T(8,128)(2,1)S(1)}, u32[]{:S(2)}, u32[]{:S(2)}) collective-permute-start(bf16[512,128]{1,0:T(8,128)(2,1)S(1)} %get-tuple-element.75), channel_id=1, source_target_pairs={{0,16},{8,24},{16,0},{24,8},{1,17},{9,25},{17,1},{25,9},{2,18},{10... | collective-permute-start | bytes 393224 | tf_op jit(solution)/shard_map/ppermute | solution.py:458
  175.3 11.0 %collective-permute-start.21 = (bf16[512,128]{1,0:T(8,128)(2,1)S(1)}, bf16[512,128]{1,0:T(8,128)(2,1)S(1)}, u32[]{:S(2)}, u32[]{:S(2)}) collective-permute-start(bf16[512,128]{1,0:T(8,128)(2,1)S(1)} %get-tuple-element.76), channel_id=1, source_target_pairs={{0,8},{8,16},{16,24},{24,0},{1,9},{9,17},{17,25},{25,1},{2,10},{10... | collective-permute-start | bytes 393224 | tf_op jit(solution)/shard_map/ppermute | solution.py:458
  176.2 15.0 %collective-permute-start.26 = (bf16[512,128]{1,0:T(8,128)(2,1)S(1)}, bf16[512,128]{1,0:T(8,128)(2,1)S(1)}, u32[]{:S(2)}, u32[]{:S(2)}) collective-permute-start(bf16[512,128]{1,0:T(8,128)(2,1)S(1)} %get-tuple-element.70), channel_id=1, source_target_pairs={{0,24},{8,0},{16,8},{24,16},{1,25},{9,1},{17,9},{25,17},{2,26},{10... | collective-permute-start | bytes 393224 | tf_op jit(solution)/shard_map/ppermute | solution.py:458
  178.7 12.6 %collective-permute-start.25 = (bf16[512,128]{1,0:T(8,128)(2,1)S(1)}, bf16[512,128]{1,0:T(8,128)(2,1)S(1)}, u32[]{:S(2)}, u32[]{:S(2)}) collective-permute-start(bf16[512,128]{1,0:T(8,128)(2,1)S(1)} %get-tuple-element.71), channel_id=1, source_target_pairs={{0,16},{8,24},{16,0},{24,8},{1,17},{9,25},{17,1},{25,9},{2,18},{10... | collective-permute-start | bytes 393224 | tf_op jit(solution)/shard_map/ppermute | solution.py:458
  180.9 10.4 %collective-permute-start.24 = (bf16[512,128]{1,0:T(8,128)(2,1)S(1)}, bf16[512,128]{1,0:T(8,128)(2,1)S(1)}, u32[]{:S(2)}, u32[]{:S(2)}) collective-permute-start(bf16[512,128]{1,0:T(8,128)(2,1)S(1)} %get-tuple-element.72), channel_id=1, source_target_pairs={{0,8},{8,16},{16,24},{24,0},{1,9},{9,17},{17,25},{25,1},{2,10},{10... | collective-permute-start | bytes 393224 | tf_op jit(solution)/shard_map/ppermute | solution.py:458
  (30 other events, 128.3 us)
where the time goes:
time: 195 us
  Pallas kernels  75.7 us (39%)
  starting transfers between devices  55.1 us (28%)
  waiting for transfers between devices  40.9 us (21%)
  local copies, waits for them, and re-layouts  21.3 us (11%)
    pallas_call x12, Pallas kernels, call(): pl.pallas_call(body, out_shape=outs, in_specs=[SMEM] * smem + [VM] * (len...  75.7 us
    ppermute x27, starting transfers between devices, shift(): return lax.ppermute(value, axis, [(i, (i + step) % 4) for i in range(4)])  41 us
    ppermute x27, waiting for transfers between devices, shift(): return lax.ppermute(value, axis, [(i, (i + step) % 4) for i in range(4)])  27.7 us
    all_to_all x3, starting transfers between devices, to_all(): lax.all_to_all(copies, ('y', 'head'), split_axis=0, concat_axis=0, tiled=...  14.1 us
    all_to_all x3, waiting for transfers between devices, to_all(): lax.all_to_all(copies, ('y', 'head'), split_axis=0, concat_axis=0, tiled=...  13.2 us
    unnamed x67, local copies, waits for them, and re-layouts  9.23 us
    squeeze x6, local copies, waits for them, and re-layouts, y_exchange(): slots[3]  7.77 us
  transfers between devices with their start and end apart: 30, of which 10 were waited for; matrix products, arithmetic and copies ran while one was open for 6% of the time, Pallas kernels for 22%

commit v1 on v0

v1 whole, which is shorter than its diff:
```python
import math

import jax
import jax.numpy as jnp
from jax import lax
from jax.experimental import pallas as pl
from jax.experimental.pallas import tpu as pltpu
from jax.sharding import Mesh
from jax.sharding import PartitionSpec as P

DH = 128
D = 4096
SEG = 512
EPSILON = 1e-06
FLOOR = -1e30
SCALE = 1.0 / math.sqrt(DH)
F32 = jnp.float32
BF16 = jnp.bfloat16


def nt(a, b):
    return lax.dot_general(a, b, (((1,), (1,)), ((), ())), preferred_element_type=F32)


def nn(a, b):
    return lax.dot_general(a, b, (((1,), (0,)), ((), ())), preferred_element_type=F32)


def tn(a, b):
    return lax.dot_general(a, b, (((0,), (0,)), ((), ())), preferred_element_type=F32)


def order_matrix(transposed):
    row = lax.broadcasted_iota(jnp.int32, (SEG, SEG), 1 if transposed else 0)
    col = lax.broadcasted_iota(jnp.int32, (SEG, SEG), 0 if transposed else 1)
    rb = row >> 6
    residue = ((rb & 1) << 2) | (rb & 2) | (rb >> 2)
    return (col == ((row & 63) * 8 + residue)).astype(F32).astype(BF16)


def slab(index):
    return pl.ds(pl.multiple_of(index * DH, DH), DH)


SMEM = pl.BlockSpec(memory_space=pltpu.SMEM)
VM = pl.BlockSpec(memory_space=pltpu.VMEM)


def call(body, ins, smem, outs, scratch=(), flops=0, far=(), rows=None, room=24):
    return call_inner(body, ins, smem, outs, scratch, flops, far, rows, room)


def call_inner(body, ins, smem, outs, scratch, flops, far, rows, room):
    specs = [SMEM] * smem + [VM] * (len(ins) - smem)
    for i in far:
        specs[i] = pl.BlockSpec(memory_space=pl.ANY)
    for i, at in (rows or {}).items():
        shape = (1, *ins[i].shape[1:])
        specs[i] = pl.BlockSpec(shape, lambda *_, at=at: (at, 0, 0, 0, 0))
    return pl.pallas_call(
        body,
        out_shape=outs,
        grid=(1,) if rows else (),
        in_specs=specs,
        out_specs=jax.tree.map(lambda _: VM, outs),
        scratch_shapes=list(scratch),
        compiler_params=pltpu.CompilerParams(vmem_limit_bytes=room << 20),
        cost_estimate=pl.CostEstimate(flops=flops, transcendentals=0, bytes_accessed=4 << 20),
    )(*ins)


def S(shape, dtype):
    return jax.ShapeDtypeStruct(shape, dtype)


def ordered_slots(y, order, ref, outs):
    ones = jnp.ones((8, DH), BF16)
    squares = jnp.zeros((8, SEG), F32)
    for s in range(4):
        x = nn(order, ref[:, slab((y + s) % 4)])
        outs[s][...] = x.astype(BF16)
        square = x * x
        high = square.astype(BF16)
        low = (square - high.astype(F32)).astype(BF16)
        squares = squares + nt(ones, high) + nt(ones, low)
    return squares


def prep_v_kernel(ids, v, o0, o1, o2, o3):
    order = order_matrix(False)
    for s, out in enumerate((o0, o1, o2, o3)):
        out[...] = nn(order, v[:, slab((ids[1] + s) % 4)]).astype(BF16)


def prep_k_kernel(ids, k, o0, o1, o2, o3, sums_out):
    sums_out[...] = ordered_slots(ids[1], order_matrix(False), k, (o0, o1, o2, o3))


def prep_qg_kernel(ids, q, g, key_sums, o0, o1, o2, o3, stats_out):
    y = ids[1]
    order = order_matrix(False)
    outs = (o0, o1, o2, o3)
    sums = ordered_slots(y, order, q, [out.at[0] for out in outs])
    both = jnp.concatenate([sums[0:1], key_sums[0:1]], axis=0)
    for i in range(32):
        stats_out[i] = both
    for s in range(4):
        outs[s][1] = nn(order, g[:, slab((y + s) % 4)]).astype(BF16)


def total_rows(ref, first, count, which):
    total = ref[first, which : which + 1]
    for i in range(1, count):
        total = total + ref[first + i, which : which + 1]
    return total


def inverse_row(stats, c, which):
    return lax.rsqrt(total_rows(stats, 8 * c, 8, which) / D + EPSILON)


def normed(raw, inverse, gain):
    t = jnp.transpose(raw.astype(F32)) * inverse * gain
    return jnp.transpose(t).astype(BF16)


def place_v_kernel(ids, p0, p1, p2, p3, out):
    y = ids[1]
    for s, piece in enumerate((p0, p1, p2, p3)):
        out[(y + 4 - s) % 4] = piece[...].reshape(4, 128, DH)


def gain_column(ids, gain):
    row = gain[:, slab(ids[1])].astype(F32)
    return jnp.transpose(jnp.broadcast_to(row, (DH, DH)))[:, 0:1]


def norm_k_kernel(ids, p0, p1, p2, p3, stats, gain, out):
    y = ids[1]
    scale = gain_column(ids, gain)
    for s, piece in enumerate((p0, p1, p2, p3)):
        c = (y + 4 - s) % 4
        out[c] = normed(piece[...], inverse_row(stats, c, 1), scale).reshape(4, 128, DH)


def head_bits(ids):
    h = 4 * ids[2] + ids[1]
    par = h & 1
    return par, 2 * par + ((h >> 1) & 1), (h >> 2) & 1


def forward_part(keys, vals, q, score_ref, mask=None, keep=False):
    count = len(keys)
    top = None
    for j in range(count):
        s = nt(keys[j](), q) * SCALE
        score_ref[j] = s
        t = jnp.max(s, axis=0, keepdims=True)
        top = t if top is None else jnp.maximum(top, t)
    if mask is not None:
        top = jnp.where(mask, top, FLOOR)
    total, summed = None, None
    for j in range(count):
        w = jnp.exp(score_ref[j] - top)
        if mask is not None:
            w = jnp.where(mask, w, 0.0)
        if keep:
            score_ref[j] = w
        t = jnp.sum(w, axis=0, keepdims=True)
        a = tn(vals[j](), w.astype(BF16))
        total = t if total is None else total + t
        summed = a if summed is None else summed + a
    return top, total, summed


def merge(m_ref, l_ref, a_ref, at, top, total, summed):
    m = m_ref[at]
    new = jnp.maximum(m, top)
    old_f = jnp.exp(m - new)
    new_f = jnp.exp(top - new)
    m_ref[at] = new
    l_ref[at] = old_f * l_ref[at] + new_f * total
    a_ref[at] = old_f * a_ref[at] + new_f * summed


def cut(x, b):
    return x[:, b * 128 : (b + 1) * 128]


def rows_of(ref, spots):
    return jnp.concatenate([ref[c, b] for c, b in spots], axis=0)


def chunks_of(ref, spots):
    return [lambda at=spots[i : i + PER]: rows_of(ref, at) for i in range(0, len(spots), PER)]


def level_forward_kernel(ids, p0, p1, p2, p3, stats, gain, k, v, q, g, m_out, l_out, a_out, score):
    y = ids[1]
    par, quarter, _ = head_bits(ids)
    scale = gain_column(ids, gain)
    for s, piece in enumerate((p0, p1, p2, p3)):
        c = (y + 4 - s) % 4
        q[c] = normed(piece[0], inverse_row(stats, c, 0), scale).reshape(4, 128, DH)
        g[c] = piece[1].reshape(4, 128, DH)

    def level0(c, carry):
        spots = [(c, b) for b in range(4)]
        top, total, summed = forward_part(
            chunks_of(k, spots), chunks_of(v, spots), rows_of(q, spots), score
        )
        for b in range(4):
            m_out[c, b] = cut(top, b)
            l_out[c, b] = cut(total, b)
            a_out[c, b] = cut(summed, b)
        return carry

    lax.fori_loop(0, 4, level0, 0)

    def joined(spots):
        top, total, summed = forward_part(
            chunks_of(k, spots), chunks_of(v, spots), rows_of(q, spots), score
        )
        for i, at in enumerate(spots):
            merge(m_out, l_out, a_out, at, cut(top, i), cut(total, i), cut(summed, i))

    def level1(s, carry):
        joined([(2 * s + i // 2, 2 * par + i % 2) for i in range(4)])
        return carry

    lax.fori_loop(0, 2, level1, 0)
    joined([(i, quarter) for i in range(4)])


def backward_chunk(key, val, q, g, lse, delta, mask=None):
    soft = jnp.exp(nt(key, q) * SCALE - lse)
    if mask is not None:
        soft = jnp.where(mask, soft, 0.0)
    grad = (soft * (nt(val, g) - delta)).astype(BF16)
    return tn(key, grad), nn(grad, q) * SCALE, nn(soft.astype(BF16), g)


def place(ids, lists, c, j):
    block = lists[j, 4 * ids[0] + c]
    owner = block // 4
    return ((owner // 4) + 4 - ids[0]) % 4, owner % 4, block % 4


def runs(lb):
    return [(rb // 2, pl.ds(pl.multiple_of((rb % 2) * 64 + lb * 16, 16), 16)) for rb in range(8)]


def level3_spots(ids):
    _, quarter, half = head_bits(ids)
    halves = pl.ds(pl.multiple_of(half * 64, 64), 64)
    mask = (lax.broadcasted_iota(jnp.int32, (1, SEG), 1) % 128) // 64 == half
    partner = jnp.where(ids[0] % 2 == 0, 1, 3)
    return quarter, halves, mask, partner


def quarter_row(ref, c, quarter):
    out = cut(ref[c], 0)
    for i in range(1, 4):
        out = jnp.where(quarter == i, cut(ref[c], i), out)
    return out


def kept_part(w, factor, key, val, q, g, delta):
    soft = w * factor
    grad = (soft * (nt(val, g) - delta)).astype(BF16)
    return tn(key, grad), nn(grad, q) * SCALE, nn(soft.astype(BF16), g)


def main_kernel(
    ids, lists, q, g, k0, v0, k1, v1, k2, v2, k3, v3, m_in, l_in, a_in,
    att, dq, lse_out, delta_out, dk_own, dv_own, v_up, v_down, k_up, k_down, vp, vn, kp, kn,
    kall, vall, dk, dv, score, score3, m, l, a, sems,
):
    quarter, halves, mask, partner = level3_spots(ids)
    copies = [
        pltpu.make_async_copy(src, dst.at[i], sems.at[n, i])
        for n, (dst, group) in enumerate(((kall, (k0, k1, k2, k3)), (vall, (v0, v1, v2, v3))))
        for i, src in enumerate(group)
    ]
    for copy in copies:
        copy.start()
    m[...] = m_in[...]
    l[...] = l_in[...]
    a[...] = a_in[...]
    dk[...] = jnp.zeros(dk.shape, F32)
    dv[...] = jnp.zeros(dv.shape, F32)
    for copy in copies:
        copy.wait()

    spots3 = [(at, c, quarter, halves) for at in (0, partner) for c in range(4)]
    rows3 = [(c, quarter) for c in range(4)]

    def eight(ref):
        return jnp.concatenate([ref[at] for at in spots3], axis=0)

    top3, total, summed = forward_part(
        [lambda: eight(kall)], [lambda: eight(vall)], rows_of(q, rows3), score3, mask, True
    )
    for i in range(4):
        merge(m, l, a, (i, quarter), cut(top3, i), cut(total, i), cut(summed, i))

    def one_ctx(c, carry):
        rows = q[c].reshape(SEG, DH)
        grows = g[c].reshape(SEG, DH)
        groups = []
        for i in (0, 4):
            spots = []
            for j in range(i, i + 4):
                rel, cc, lb = place(ids, lists, c, j)
                spots += [(rel, cc, b, r) for b, r in runs(lb)]
            groups.append(spots)

        def blocks(ref):
            return [lambda at=at: jnp.concatenate([ref[x] for x in at], axis=0) for at in groups]

        keys, vals = blocks(kall), blocks(vall)
        top, total, summed = forward_part(keys, vals, rows, score, None, True)
        for b in range(4):
            merge(m, l, a, (c, b), cut(top, b), cut(total, b), cut(summed, b))
        joint = jnp.concatenate([m[c, b] for b in range(4)], axis=1)
        whole = jnp.concatenate([l[c, b] for b in range(4)], axis=1)
        merged = jnp.concatenate([a[c, b] for b in range(4)], axis=1) / whole
        att[c] = merged.astype(BF16)
        lse = joint + jnp.log(whole)
        delta = jnp.sum(jnp.transpose(grows.astype(F32)) * merged, axis=0, keepdims=True)
        lse_out[c] = lse
        delta_out[c] = delta
        factor = jnp.exp(top - lse)
        grad_q = None
        for n, spots in enumerate(groups):
            gq, gk, gv = kept_part(score[n], factor, keys[n](), vals[n](), rows, grows, delta)
            grad_q = gq if grad_q is None else grad_q + gq
            gk = gk.astype(BF16).astype(F32)
            gv = gv.astype(BF16).astype(F32)
            for i, spot in enumerate(spots):
                dk[spot] = dk[spot] + gk[16 * i : 16 * (i + 1)]
                dv[spot] = dv[spot] + gv[16 * i : 16 * (i + 1)]
        for b in range(4):
            dq[c, b] = cut(grad_q, b) * SCALE
        return carry

    lax.fori_loop(0, 4, one_ctx, 0)
    logs = jnp.concatenate([quarter_row(lse_out, c, quarter) for c in range(4)], axis=1)
    deltas = jnp.concatenate([quarter_row(delta_out, c, quarter) for c in range(4)], axis=1)
    gq, gk, gv = kept_part(
        score3[0], jnp.exp(top3 - logs), eight(kall), eight(vall), rows_of(q, rows3), rows_of(g, rows3), deltas
    )
    for c in range(4):
        dq[c, quarter] = dq[c, quarter] + cut(gq, c) * SCALE
    for n, spot in enumerate(spots3):
        dk[spot] = dk[spot] + gk[64 * n : 64 * (n + 1)]
        dv[spot] = dv[spot] + gv[64 * n : 64 * (n + 1)]
    dk_own[...] = dk[0]
    dv_own[...] = dv[0]
    for ref, up, down, up_kept, down_kept in ((dv, v_up, v_down, vp, vn), (dk, k_up, k_down, kp, kn)):
        up[0] = ref[2, 0:2].astype(BF16)
        up[1] = ref[1, 2:4].astype(BF16)
        down[0] = ref[2, 2:4].astype(BF16)
        down[1] = ref[3, 0:2].astype(BF16)
        up_kept[...] = ref[1, 0:2]
        down_kept[...] = ref[3, 2:4]


def relay_kernel(up, down, from_below, from_above, up_out, down_out):
    up_out[...] = (up[...] + from_below[0].astype(F32)).astype(BF16)
    down_out[...] = (down[...] + from_above[0].astype(F32)).astype(BF16)


def put_pair(out, x):
    high = x.astype(BF16)
    out[0] = high
    out[1] = (x - high.astype(F32)).astype(BF16)


def main3_kernel(
    ids, q, g, k, v, lse, delta, dq_in, dk_in, dv_in, p0, p1, p2, p3, gain, att,
    dk, dv, a0, a1, a2, a3, s_out, dq,
):
    y = ids[1]
    par, quarter, _ = head_bits(ids)
    dq[...] = dq_in[...]
    dk[...] = dk_in[...]
    dv[...] = dv_in[...]

    def part(spots, rows, grows, logs, deltas):
        for i in range(0, 4, PER):
            at = spots[i : i + PER]
            gq, gk, gv = backward_chunk(rows_of(k, at), rows_of(v, at), rows, grows, logs, deltas)
            for n, (c, b) in enumerate(at):
                dk[c, b] = dk[c, b] + gk[128 * n : 128 * (n + 1)]
                dv[c, b] = dv[c, b] + gv[128 * n : 128 * (n + 1)]
            for n, (c, b) in enumerate(spots):
                dq[c, b] = dq[c, b] + cut(gq, n) * SCALE

    def gather(spots):
        return (
            rows_of(q, spots),
            rows_of(g, spots),
            jnp.concatenate([quarter_row(lse, c, b) for c, b in spots], axis=1),
            jnp.concatenate([quarter_row(delta, c, b) for c, b in spots], axis=1),
        )

    def level0(c, carry):
        part([(c, b) for b in range(4)], q[c].reshape(SEG, DH), g[c].reshape(SEG, DH), lse[c], delta[c])
        return carry

    lax.fori_loop(0, 4, level0, 0)

    def level1(s, carry):
        spots = [(2 * s + i // 2, 2 * par + i % 2) for i in range(4)]
        part(spots, *gather(spots))
        return carry

    lax.fori_loop(0, 2, level1, 0)
    spots = [(i, quarter) for i in range(4)]
    part(spots, *gather(spots))
    pieces = (p0, p1, p2, p3)
    scale = gain_column(ids, gain)
    for s, out in enumerate((a0, a1, a2, a3)):
        c = (y + s) % 4
        raw = jnp.transpose(pieces[(4 - s) % 4][0].astype(F32))
        adj = jnp.concatenate([dq[c, b] for b in range(4)], axis=1) * scale
        put_pair(out, adj)
        out[2] = att[c]
        inner = jnp.sum(raw * adj, axis=0, keepdims=True)
        for h in range(8):
            s_out[8 * c + h] = inner


def add_rows(own, below1, above1, below2, above2, total):
    total[0:2] = own[0:2] + below2[...].astype(F32) + above1[0].astype(F32)
    total[2:4] = own[2:4] + below1[0].astype(F32) + above2[...].astype(F32)


def collect_v_kernel(ids, dv, below1, above1, below2, above2, o0, o1, o2, o3, total):
    add_rows(dv, below1, above1, below2, above2, total)
    for s, out in enumerate((o0, o1, o2, o3)):
        out[...] = jnp.transpose(total[(ids[1] + s) % 4].reshape(SEG, DH)).astype(BF16)


def collect_k_kernel(
    ids, dk, below1, above1, below2, above2, p0, p1, p2, p3, gain,
    o0, o1, o2, o3, s_out, total,
):
    add_rows(dk, below1, above1, below2, above2, total)
    pieces = (p0, p1, p2, p3)
    scale = gain_column(ids, gain)
    for s, out in enumerate((o0, o1, o2, o3)):
        c = (ids[1] + s) % 4
        raw = jnp.transpose(pieces[(4 - s) % 4][...].astype(F32))
        adj = jnp.transpose(total[c].reshape(SEG, DH)) * scale
        put_pair(out, adj)
        inner = jnp.sum(raw * adj, axis=0, keepdims=True)
        for h in range(8):
            s_out[8 * c + h] = inner


def restore_kernel(ids, p0, p1, p2, p3, out):
    y = ids[1]
    order = order_matrix(True)
    for s, piece in enumerate((p0, p1, p2, p3)):
        out[:, slab((y + 4 - s) % 4)] = nt(order, piece[...]).astype(BF16)


def finish_kernel(which, ids, inner, stats, raw, p0, p1, p2, p3, out, plain=None):
    y = ids[1]
    order = order_matrix(True)
    total = total_rows(inner, 0, 32, 0)
    r = inverse_row(stats, y, which)
    for s, piece in enumerate((p0, p1, p2, p3)):
        at = slab((y + 4 - s) % 4)
        x = tn(raw[:, at], order)
        adj = piece[0].astype(F32) + piece[1].astype(F32)
        grads = (r * adj - x * (r * r * r) * total / D).astype(BF16)
        out[:, at] = nt(order, grads).astype(BF16)
        if plain is not None:
            plain[:, at] = nt(order, piece[2]).astype(BF16)


def shift(value, axis, step):
    return lax.ppermute(value, axis, [(i, (i + step) % 4) for i in range(4)])


def y_exchange(slots):
    far = shift(slots[2], "y", 2)
    return [slots[0], shift(slots[1], "y", 1), far, shift(slots[3], "y", -1)]


def to_all(copies):
    return lax.all_to_all(copies, ("y", "head"), split_axis=0, concat_axis=0, tiled=True)


def shards_inner(queries, key_states, values, query_gain, key_gain, memory_blocks, cotangent):
    z, y, hd = lax.axis_index("z"), lax.axis_index("y"), lax.axis_index("head")
    ids = jnp.stack([z, y, hd]).astype(jnp.int32)

    q_gain, k_gain = query_gain.reshape(1, 4 * DH), key_gain.reshape(1, 4 * DH)
    lists = memory_blocks.T
    head4 = (4, 4, 128, DH)
    one, full = S(head4, BF16), S(head4, F32)
    slot = S((2, SEG, DH), BF16)
    back = S((3, DH, SEG), BF16)
    every = S((32, 1, SEG), F32)
    row, row4 = S((4, 1, SEG), F32), S((4, 4, 1, 128), F32)
    flat = S((SEG, 4 * DH), BF16)

    part = S((SEG, DH), BF16)
    v_slots = call(prep_v_kernel, (ids, values), 1, (part,) * 4)
    v_pieces = y_exchange(v_slots)
    *k_slots, sums = call(prep_k_kernel, (ids, key_states), 1, (part,) * 4 + (S((8, SEG), F32),))
    k_pieces = y_exchange(k_slots)
    *qg, sums = call(
        prep_qg_kernel, (ids, queries, cotangent, sums), 1, (slot,) * 4 + (S((32, 2, SEG), F32),)
    )
    stats = to_all(sums)
    qg_pieces = y_exchange(qg)
    v0 = call(place_v_kernel, (ids, *v_pieces), 1, one)
    v3, v1 = shift(v0, "z", 1), shift(v0, "z", -1)
    k0 = call(norm_k_kernel, (ids, *k_pieces, stats, k_gain), 1, one)
    k3, k1 = shift(k0, "z", 1), shift(k0, "z", -1)
    v2 = shift(v1, "z", -1)
    k2 = shift(k3, "z", 1)
    q, g, m, l, a = call(
        level_forward_kernel,
        (ids, *qg_pieces, stats, q_gain, k0, v0),
        1,
        (one, one, row4, row4, full),
        [pltpu.VMEM((4 // PER, 128 * PER, SEG), F32)],
        flops=7 * 2 * 2 * 512 * 512 * 128,
    )
    half, kept = S((2, 2, 4, 128, DH), BF16), S((2, 4, 128, DH), F32)
    att, dq, lse, delta, dk, dv, v_up, v_down, k_up, k_down, vp, vn, kp, kn = call(
        main_kernel,
        (ids, lists, q, g, k0, v0, k1, v1, k2, v2, k3, v3, m, l, a),
        2,
        (S((4, DH, SEG), BF16), full, row, row, full, full) + (half,) * 4 + (kept,) * 4,
        [
            pltpu.VMEM((4, *head4), BF16),
            pltpu.VMEM((4, *head4), BF16),
            pltpu.VMEM((4, *head4), F32),
            pltpu.VMEM((4, *head4), F32),
            pltpu.VMEM((2, SEG, SEG), F32),
            pltpu.VMEM((1, SEG, SEG), F32),
            pltpu.VMEM((4, 4, 1, 128), F32),
            pltpu.VMEM((4, 4, 1, 128), F32),
            pltpu.VMEM(head4, F32),
            pltpu.SemaphoreType.DMA((2, 4)),
        ],
        flops=9 * 6 * 2 * 512 * 512 * 128,
        far=range(4, 12),
        room=44,
    )
    v_below, v_above = shift(v_up, "z", 1), shift(v_down, "z", -1)
    k_below, k_above = shift(k_up, "z", 1), shift(k_down, "z", -1)
    dk, dv, *q_slots, q_s = call(
        main3_kernel,
        (ids, q, g, k0, v0, lse, delta, dq, dk, dv, *qg_pieces, q_gain, att),
        1,
        (full, full) + (back,) * 4 + (every,),
        [pltpu.VMEM(head4, F32)],
        flops=7 * 5 * 2 * 512 * 512 * 128,
    )

    def relayed(up, down, below, above):
        pair = S((2, 4, 128, DH), BF16)
        rows = {2: 0, 3: 0}
        return call(relay_kernel, (up, down, below, above), 0, (pair, pair), rows=rows)

    v_up, v_down = relayed(vp, vn, v_below, v_above)
    v_below2, v_above2 = shift(v_up, "z", 1), shift(v_down, "z", -1)
    k_up, k_down = relayed(kp, kn, k_below, k_above)
    k_below2, k_above2 = shift(k_up, "z", 1), shift(k_down, "z", -1)
    q_adj = y_exchange(q_slots)
    q_inner = to_all(q_s)
    v_slots = call(
        collect_v_kernel,
        (ids, dv, v_below, v_above, v_below2, v_above2),
        1,
        (S((DH, SEG), BF16),) * 4,
        [pltpu.VMEM(head4, F32)],
        rows={2: 1, 3: 1},
    )
    v_back = y_exchange(v_slots)
    query_grads, attended = call(
        lambda *refs: finish_kernel(0, *refs),
        (ids, q_inner, stats, queries, *q_adj),
        1,
        (flat, flat),
    )
    value_grads = call(restore_kernel, (ids, *v_back), 1, flat)
    *k_slots, k_s = call(
        collect_k_kernel,
        (ids, dk, k_below, k_above, k_below2, k_above2, *k_pieces, k_gain),
        1,
        (S((2, DH, SEG), BF16),) * 4 + (every,),
        [pltpu.VMEM(head4, F32)],
        rows={2: 1, 3: 1},
    )
    k_adj = y_exchange(k_slots)
    k_inner = to_all(k_s)
    key_grads = call(
        lambda *refs: finish_kernel(1, *refs), (ids, k_inner, stats, key_states, *k_adj), 1, flat
    )
    return (attended, query_grads, key_grads, value_grads)


PER = 4


def solution(mesh):
    split = Mesh(mesh.devices.reshape(4, 4, 8), ("z", "y", "head"))
    big = P(("z", "y"), "head")
    in_specs = (big, big, big, P("head"), P("head"), P(), big)
    return jax.shard_map(
        shards_inner, mesh=split, in_specs=in_specs, out_specs=(big, big, big, big), check_vma=False
    )
```

time: 195 us -> 171 us (0.88)
  Pallas kernels: 75.7 us -> 48.1 us
  local copies, waits for them, and re-layouts: 21.3 us -> 8.51 us
  blocking collectives: 0 us -> 11.7 us
  starting transfers between devices: 55.1 us -> 62.2 us
  waiting for transfers between devices: 40.9 us -> 38.2 us
    pallas_call x12 -> x15, Pallas kernels: 75.7 us -> 48.1 us  [call_inner(): pl.pallas_call(body, out_shape=outs, grid=(1,) if rows else (), in_specs=...]
    all_to_all x0 -> x1, blocking collectives: none -> 11.7 us  [to_all(): lax.all_to_all(copies, ('y', 'head'), split_axis=0, concat_axis=0, tiled=...]
    ppermute x27 -> x32, starting transfers between devices: 41 us -> 51.3 us  [shift(): return lax.ppermute(value, axis, [(i, (i + step) % 4) for i in range(4)])]
    all_to_all x3 -> x2, waiting for transfers between devices: 13.2 us -> 4.47 us  [to_all(): lax.all_to_all(copies, ('y', 'head'), split_axis=0, concat_axis=0, tiled=...]
    squeeze x6 -> x0, local copies, waits for them, and re-layouts: 7.77 us -> none  [y_exchange(): slots[3]]
    ppermute x27 -> x32, waiting for transfers between devices: 27.7 us -> 33.7 us  [shift(): return lax.ppermute(value, axis, [(i, (i + step) % 4) for i in range(4)])]
    all_to_all x3 -> x2, starting transfers between devices: 14.1 us -> 10.9 us  [to_all(): lax.all_to_all(copies, ('y', 'head'), split_axis=0, concat_axis=0, tiled=...]
    broadcast_in_dim x3 -> x0, local copies, waits for them, and re-layouts: 2.17 us -> none  [to_all(): copies = jnp.broadcast_to(value, (32, *value.shape))]
  transfers between devices with their start and end apart: 30 -> 34, of which waited for: 10 -> 9; matrix products, arithmetic and copies ran while one was open for 6% -> 0% of each run, Pallas kernels for 22% -> 17%
where the time goes in v1:
time: 171 us; the launch traced here: 170 us
  starting transfers between devices  62.2 us (36%)
  Pallas kernels  48.1 us (28%)
  waiting for transfers between devices  38.2 us (22%)
  blocking collectives  11.7 us (7%)
  local copies, waits for them, and re-layouts  8.51 us (5%)
    ppermute x32, starting transfers between devices, shift(): return lax.ppermute(value, axis, [(i, (i + step) % 4) for i in range(4)])  51.3 us
    pallas_call x15, Pallas kernels, call_inner(): pl.pallas_call(body, out_shape=outs, grid=(1,) if rows else (), in_specs=...  48.1 us
    ppermute x32, waiting for transfers between devices, shift(): return lax.ppermute(value, axis, [(i, (i + step) % 4) for i in range(4)])  33.7 us
    all_to_all x1, blocking collectives, to_all(): lax.all_to_all(copies, ('y', 'head'), split_axis=0, concat_axis=0, tiled=...  11.7 us
    all_to_all x2, starting transfers between devices, to_all(): lax.all_to_all(copies, ('y', 'head'), split_axis=0, concat_axis=0, tiled=...  10.9 us
    unnamed x48, local copies, waits for them, and re-layouts  8.5 us
    all_to_all x2, waiting for transfers between devices, to_all(): lax.all_to_all(copies, ('y', 'head'), split_axis=0, concat_axis=0, tiled=...  4.47 us
  transfers between devices with their start and end apart: 34, of which 9 were waited for; matrix products, arithmetic and copies ran while one was open for 0% of the time, Pallas kernels for 17%

profile of v1, /device:TPU:0, one launch (start us, length us, event | category | flops | bytes accessed | tf_op | source)
XLA Modules:
  0.0 169.7 jit_solution(9107017669462719194)
XLA Ops:
  4.8 2.9 %collective-permute-start.7 = (bf16[512,128]{1,0:T(8,128)(2,1)S(1)}, bf16[512,128]{1,0:T(8,128)(2,1)S(1)}, u32[]{:S(2)}, u32[]{:S(2)}) collective-permute-start(bf16[512,128]{1,0:T(8,128)(2,1)S(1)} %get-tuple-element.71), channel_id=1, source_target_pairs={{0,16},{8,24},{16,0},{24,8},{1,17},{9,25},{17,1},{25,9},{2,18},{10... | collective-permute-start | bytes 393224 | tf_op jit(solution)/shard_map/ppermute | solution.py:486
  9.1 2.2 %shard_map.102 = (bf16[512,128]{1,0:T(8,128)(2,1)S(1)}, bf16[512,128]{1,0:T(8,128)(2,1)}, bf16[512,128]{1,0:T(8,128)(2,1)}, bf16[512,128]{1,0:T(8,128)(2,1)}, f32[8,512]{1,0:T(8,128)S(1)}) custom-call(s32[3]{0:T(128)S(1)} %pad_add_fusion.ids.refs_0_, bf16[512,512]{1,0:T(8,128)(2,1)S(1)} %copy-done), custom_call_target="tpu_custom_call" | custom-call | bytes 4194304 | tf_op jit(solution)/shard_map/pallas_call | solution.py:60
  15.7 2.8 %shard_map.103 = (bf16[2,512,128]{2,1,0:T(8,128)(2,1)S(1)}, bf16[2,512,128]{2,1,0:T(8,128)(2,1)S(1)}, bf16[2,512,128]{2,1,0:T(8,128)(2,1)S(1)}, bf16[2,512,128]{2,1,0:T(8,128)(2,1)S(1)}, f32[32,2,512]{2,1,0:T(2,128)}) custom-call(s32[3]{0:T(128)S(1)} %pad_add_fusion.ids.refs_0_, bf16[512,512]{1,0:T(8,128)(2,1)S(1)} %copy-done.1, ...), custom_call_target="tpu_custom_call" | custom-call | bytes 4194304 | tf_op jit(solution)/shard_map/pallas_call | solution.py:60
  19.9 7.1 %all-to-all-start = ((f32[32,2,512]{2,1,0:T(2,128)}), f32[32,2,512]{2,1,0:T(2,128)S(1)}, u32[]{:S(2)}, u32[]{:S(2)}) async-start(f32[32,2,512]{2,1,0:T(2,128)} %get-tuple-element.64), calls=%async_computation | async-start | bytes 262144 | tf_op jit(solution)/shard_map/all_to_all | solution.py:495
  27.7 4.1 %collective-permute-start.10 = (bf16[4,4,128,128]{3,2,1,0:T(8,128)(2,1)S(1)}, bf16[4,4,128,128]{3,2,1,0:T(8,128)(2,1)S(1)}, u32[]{:S(2)}, u32[]{:S(2)}) collective-permute-start(bf16[4,4,128,128]{3,2,1,0:T(8,128)(2,1)S(1)} %shard_map.106.v.v0), channel_id=1, source_target_pairs={{0,96},{32,0},{64,32},{96,64},{1,97},{33,1},{65,33},{97,65},{2,98}... | collective-permute-start | bytes 1572872 | tf_op jit(solution)/shard_map/ppermute | solution.py:486
  31.8 3.0 %all-to-all-done.stats.refs_2_ = f32[32,2,512]{2,1,0:T(2,128)S(1)} async-done(((f32[32,2,512]{2,1,0:T(2,128)}), f32[32,2,512]{2,1,0:T(2,128)S(1)}, u32[]{:S(2)}, u32[]{:S(2)}) %all-to-all-start) | async-done | bytes 131104 | tf_op jit(solution)/shard_map/all_to_all | solution.py:495
  35.9 2.0 %collective-permute-start.11 = (bf16[4,4,128,128]{3,2,1,0:T(8,128)(2,1)S(1)}, bf16[4,4,128,128]{3,2,1,0:T(8,128)(2,1)S(1)}, u32[]{:S(2)}, u32[]{:S(2)}) collective-permute-start(bf16[4,4,128,128]{3,2,1,0:T(8,128)(2,1)S(1)} %shard_map.104.k.k0), channel_id=1, source_target_pairs={{0,32},{32,64},{64,96},{96,0},{1,33},{33,65},{65,97},{97,1},{2,34}... | collective-permute-start | bytes 1572872 | tf_op jit(solution)/shard_map/ppermute | solution.py:486
  38.5 2.0 %collective-permute-start.1 = (bf16[2,512,128]{2,1,0:T(8,128)(2,1)S(1)}, bf16[2,512,128]{2,1,0:T(8,128)(2,1)S(1)}, u32[]{:S(2)}, u32[]{:S(2)}) collective-permute-start(bf16[2,512,128]{2,1,0:T(8,128)(2,1)S(1)} %copy-done.14), channel_id=1, source_target_pairs={{0,16},{8,24},{16,0},{24,8},{1,17},{9,25},{17,1},{25,9},{2,18},{10... | collective-permute-start | bytes 786440 | tf_op jit(solution)/shard_map/ppermute | solution.py:486
  40.5 1.9 %collective-permute-start.14 = (bf16[4,4,128,128]{3,2,1,0:T(8,128)(2,1)S(1)}, bf16[4,4,128,128]{3,2,1,0:T(8,128)(2,1)S(1)}, u32[]{:S(2)}, u32[]{:S(2)}) collective-permute-start(bf16[4,4,128,128]{3,2,1,0:T(8,128)(2,1)S(1)} %shard_map.106.v.v0), channel_id=1, source_target_pairs={{0,32},{32,64},{64,96},{96,0},{1,33},{33,65},{65,97},{97,1},{2,34}... | collective-permute-start | bytes 1572872 | tf_op jit(solution)/shard_map/ppermute | solution.py:486
  42.4 10.4 %collective-permute-done.p1 = bf16[2,512,128]{2,1,0:T(8,128)(2,1)S(1)} collective-permute-done((bf16[2,512,128]{2,1,0:T(8,128)(2,1)S(1)}, bf16[2,512,128]{2,1,0:T(8,128)(2,1)S(1)}, u32[]{:S(2)}, u32[]{:S(2)}) %collective-permute-start) | collective-permute-done | bytes 262176 | tf_op jit(solution)/shard_map/ppermute | solution.py:486
  52.8 2.5 %collective-permute-start.9 = (bf16[4,4,128,128]{3,2,1,0:T(8,128)(2,1)S(1)}, bf16[4,4,128,128]{3,2,1,0:T(8,128)(2,1)S(1)}, u32[]{:S(2)}, u32[]{:S(2)}) collective-permute-start(bf16[4,4,128,128]{3,2,1,0:T(8,128)(2,1)S(1)} %shard_map.104.k.k0), channel_id=1, source_target_pairs={{0,96},{32,0},{64,32},{96,64},{1,97},{33,1},{65,33},{97,65},{2,98}... | collective-permute-start | bytes 1572872 | tf_op jit(solution)/shard_map/ppermute | solution.py:486
  57.3 6.3 %collective-permute-done.2.p3 = bf16[2,512,128]{2,1,0:T(8,128)(2,1)S(1)} collective-permute-done((bf16[2,512,128]{2,1,0:T(8,128)(2,1)S(1)}, bf16[2,512,128]{2,1,0:T(8,128)(2,1)S(1)}, u32[]{:S(2)}, u32[]{:S(2)}) %collective-permute-start.2) | collective-permute-done | bytes 262176 | tf_op jit(solution)/shard_map/ppermute | solution.py:486
  63.7 5.5 %shard_map.107 = (bf16[4,4,128,128]{3,2,1,0:T(8,128)(2,1)S(1)}, bf16[4,4,128,128]{3,2,1,0:T(8,128)(2,1)S(1)}, f32[4,4,1,128]{3,2,1,0:T(1,128)S(1)}, f32[4,4,1,128]{3,2,1,0:T(1,128)S(1)}, f32[4,4,128,128]{3,2,1,0:T(8,128)S(1)}) custom-call(s32[3]{0:T(128)S(1)} %pad_add_fusion.ids.refs_0_, bf16[2,512,128]{2,1,0:T(8,128)(2,1)S(1)} %copy-done.10, ...), custom_call_target="tpu_custom_call" | custom-call | flops 939524096 | bytes 4194304 | tf_op jit(solution)/shard_map/pallas_call | solution.py:60
  72.1 2.6 %collective-permute-done.12.k2 = bf16[4,4,128,128]{3,2,1,0:T(8,128)(2,1)S(1)} collective-permute-done((bf16[4,4,128,128]{3,2,1,0:T(8,128)(2,1)S(1)}, bf16[4,4,128,128]{3,2,1,0:T(8,128)(2,1)S(1)}, u32[]{:S(2)}, u32[]{:S(2)}) %collective-permute-start.12) | collective-permute-done | bytes 524320 | tf_op jit(solution)/shard_map/ppermute | solution.py:486
  75.4 14.5 %shard_map.108 = (bf16[4,128,512]{2,1,0:T(8,128)(2,1)S(1)}, f32[4,4,128,128]{3,2,1,0:T(8,128)}, f32[4,1,512]{2,1,0:T(1,128)S(1)}, f32[4,1,512]{2,1,0:T(1,128)S(1...) custom-call(s32[3]{0:T(128)S(1)} %pad_add_fusion.ids.refs_0_, ...), custom_call_target="tpu_custom_call" | custom-call | flops 3623878656 | bytes 4194304 | tf_op jit(solution)/shard_map/pallas_call | solution.py:60
  90.0 3.2 %collective-permute-start.26 = (bf16[2,2,4,128,128]{4,3,2,1,0:T(8,128)(2,1)S(1)}, bf16[2,2,4,128,128]{4,3,2,1,0:T(8,128)(2,1)S(1)}, u32[]{:S(2)}, u32[]{:S(2)}) collective-permute-start(bf16[2,2,4,128,128]{4,3,2,1,0:T(8,128)(2,1)S(1)} %get-tuple-element.105), channel_id=1, source_target_pairs={{0,96},{32,0},{64,32},{96,64},{1,97},{33,1},{65,33},{97,65},{2,98}... | collective-permute-start | bytes 1572872 | tf_op jit(solution)/shard_map/ppermute | solution.py:486
  93.2 3.2 %collective-permute-start.19 = (bf16[2,2,4,128,128]{4,3,2,1,0:T(8,128)(2,1)S(1)}, bf16[2,2,4,128,128]{4,3,2,1,0:T(8,128)(2,1)S(1)}, u32[]{:S(2)}, u32[]{:S(2)}) collective-permute-start(bf16[2,2,4,128,128]{4,3,2,1,0:T(8,128)(2,1)S(1)} %get-tuple-element.93), channel_id=1, source_target_pairs={{0,96},{32,0},{64,32},{96,64},{1,97},{33,1},{65,33},{97,65},{2,98}... | collective-permute-start | bytes 1572872 | tf_op jit(solution)/shard_map/ppermute | solution.py:486
  96.4 9.5 %collective-permute-done.25.from_below.below1 = bf16[2,2,4,128,128]{4,3,2,1,0:T(8,128)(2,1)S(1)} collective-permute-done((bf16[2,2,4,128,128]{4,3,2,1,0:T(8,128)(2,1)S(1)}, bf16[2,2,4,128,128]{4,3,2,1,0:T(8,128)(2,1)S(1)}, u32[]{:S(2)}, u32[]{:S(2)}) %collective-permute-start.25) | collective-permute-done | bytes 524320 | tf_op jit(solution)/shard_map/ppermute | solution.py:486
  106.5 3.0 %collective-permute-start.28 = (bf16[2,4,128,128]{3,2,1,0:T(8,128)(2,1)S(1)}, bf16[2,4,128,128]{3,2,1,0:T(8,128)(2,1)S(1)}, u32[]{:S(2)}, u32[]{:S(2)}) collective-permute-start(bf16[2,4,128,128]{3,2,1,0:T(8,128)(2,1)S(1)} %get-tuple-element.109), channel_id=1, source_target_pairs={{0,96},{32,0},{64,32},{96,64},{1,97},{33,1},{65,33},{97,65},{2,98}... | collective-permute-start | bytes 786440 | tf_op jit(solution)/shard_map/ppermute | solution.py:486
  110.7 7.4 %shard_map.109 = (f32[4,4,128,128]{3,2,1,0:T(8,128)S(1)}, f32[4,4,128,128]{3,2,1,0:T(8,128)S(1)}, bf16[3,128,512]{2,1,0:T(8,128)(2,1)S(1)}, bf16[3,128,512]{2,1,...) custom-call(s32[3]{0:T(128)S(1)} %pad_add_fusion.ids.refs_0_, ...), custom_call_target="tpu_custom_call" | custom-call | flops 2348810240 | bytes 4194304 | tf_op jit(solution)/shard_map/pallas_call | solution.py:60
  119.0 2.0 %collective-permute-start.16 = (bf16[3,128,512]{2,1,0:T(8,128)(2,1)S(1)}, bf16[3,128,512]{2,1,0:T(8,128)(2,1)S(1)}, u32[]{:S(2)}, u32[]{:S(2)}) collective-permute-start(bf16[3,128,512]{2,1,0:T(8,128)(2,1)S(1)} %get-tuple-element.87), channel_id=1, source_target_pairs={{0,16},{8,24},{16,0},{24,8},{1,17},{9,25},{17,1},{25,9},{2,18},{10... | collective-permute-start | bytes 1179656 | tf_op jit(solution)/shard_map/ppermute | solution.py:486
  122.5 3.2 %collective-permute-start.21 = (bf16[2,4,128,128]{3,2,1,0:T(8,128)(2,1)S(1)}, bf16[2,4,128,128]{3,2,1,0:T(8,128)(2,1)S(1)}, u32[]{:S(2)}, u32[]{:S(2)}) collective-permute-start(bf16[2,4,128,128]{3,2,1,0:T(8,128)(2,1)S(1)} %get-tuple-element.97), channel_id=1, source_target_pairs={{0,96},{32,0},{64,32},{96,64},{1,97},{33,1},{65,33},{97,65},{2,98}... | collective-permute-start | bytes 786440 | tf_op jit(solution)/shard_map/ppermute | solution.py:486
  127.4 2.7 %collective-permute-done.20.below2 = bf16[2,4,128,128]{3,2,1,0:T(8,128)(2,1)S(1)} collective-permute-done((bf16[2,4,128,128]{3,2,1,0:T(8,128)(2,1)S(1)}, bf16[2,4,128,128]{3,2,1,0:T(8,128)(2,1)S(1)}, u32[]{:S(2)}, u32[]{:S(2)}) %collective-permute-start.20) | collective-permute-done | bytes 262176 | tf_op jit(solution)/shard_map/ppermute | solution.py:486
  130.8 2.0 %shard_map.112 = (bf16[2,128,512]{2,1,0:T(8,128)(2,1)S(1)}, bf16[2,128,512]{2,1,0:T(8,128)(2,1)}, bf16[2,128,512]{2,1,0:T(8,128)(2,1)}, bf16[2,128,512]{2,1,0:T(8,128)(2,1)}, f32[32,1,512]{2,1,0:T(1,128)S(1)}) custom-call(s32[3]{0:T(128)S(1)} %pad_add_fusion.ids.refs_0_, f32[4,4,128,128]{3,2,1,0:T(8,128)S(1)} %get-tuple-element.91.dk, ...), custom_call_target="tpu_custom_call" | custom-call | bytes 4194304 | tf_op jit(solution)/shard_map/pallas_call | solution.py:60
  135.6 2.5 %collective-permute-start.23 = (bf16[2,128,512]{2,1,0:T(8,128)(2,1)}, bf16[2,128,512]{2,1,0:T(8,128)(2,1)S(1)}, u32[]{:S(2)}, u32[]{:S(2)}) collective-permute-start(bf16[2,128,512]{2,1,0:T(8,128)(2,1)} %get-tuple-element.101), channel_id=1, source_target_pairs={{0,16},{8,24},{16,0},{24,8},{1,17},{9,25},{17,1},{25,9},{2,18},{10... | collective-permute-start | bytes 786440 | tf_op jit(solution)/shard_map/ppermute | solution.py:486
  138.5 2.3 %collective-permute-start.30 = (bf16[128,512]{1,0:T(8,128)(2,1)}, bf16[128,512]{1,0:T(8,128)(2,1)}, u32[]{:S(2)}, u32[]{:S(2)}) collective-permute-start(bf16[128,512]{1,0:T(8,128)(2,1)} %get-tuple-element.112), channel_id=1, source_target_pairs={{0,16},{8,24},{16,0},{24,8},{1,17},{9,25},{17,1},{25,9},{2,18},{10... | collective-permute-start | bytes 393224 | tf_op jit(solution)/shard_map/ppermute | solution.py:486
  141.5 2.2 %collective-permute-start.31 = (bf16[128,512]{1,0:T(8,128)(2,1)}, bf16[128,512]{1,0:T(8,128)(2,1)}, u32[]{:S(2)}, u32[]{:S(2)}) collective-permute-start(bf16[128,512]{1,0:T(8,128)(2,1)} %get-tuple-element.113), channel_id=1, source_target_pairs={{0,24},{8,0},{16,8},{24,16},{1,25},{9,1},{17,9},{25,17},{2,26},{10... | collective-permute-start | bytes 393224 | tf_op jit(solution)/shard_map/ppermute | solution.py:486
  143.7 11.7 %all_to_all.15.refs_1_ = f32[32,1,512]{2,1,0:T(1,128)S(1)} all-to-all(f32[32,1,512]{2,1,0:T(1,128)S(1)} %get-tuple-element.84), channel_id=1, replica_groups=mesh['z'=4,'y'=4,'head'=8] {'y','head'}, dimensions={0} | all-to-all | bytes 131072 | tf_op jit(solution)/shard_map/all_to_all | solution.py:495
  155.4 3.8 %all-to-all-start.2 = ((f32[32,1,512]{2,1,0:T(1,128)}), f32[32,1,512]{2,1,0:T(1,128)S(1)}, u32[]{:S(2)}, u32[]{:S(2)}) async-start(f32[32,1,512]{2,1,0:T(1,128)} %copy-done.8), calls=%async_computation.2 | async-start | bytes 131072 | tf_op jit(solution)/shard_map/all_to_all | solution.py:495
  159.2 3.4 %shard_map.110 = (bf16[512,512]{1,0:T(8,128)(2,1)}, bf16[512,512]{1,0:T(8,128)(2,1)}) custom-call(s32[3]{0:T(128)S(1)} %pad_add_fusion.ids.refs_0_, f32[32,1,512]{2,1,0:T(1,128)S(1)} %all_to_all.15.refs_1_, f32[32,2,512]{2,1,0:T(2,128)S(1)} %all-to-all-done.stats.refs_2_, bf16[512,512]{1,0:T(8,128)(2,1)S(1)} %copy-done.1, ...), custom_call_target="tpu_custom_call" | custom-call | bytes 4194304 | tf_op jit(solution)/shard_map/pallas_call | solution.py:60
  162.7 2.6 %shard_map.116 = bf16[512,512]{1,0:T(8,128)(2,1)} custom-call(s32[3]{0:T(128)S(1)} %pad_add_fusion.ids.refs_0_, bf16[128,512]{1,0:T(8,128)(2,1)S(1)} %get-tuple-element.110.p0, bf16[128,512]{1,0:T(8,128)(2,1)S(1)} %copy-done.7, bf16[128,512]{1,0:T(8,128)(2,1)} %collective-permute-done.30.p2, bf16[128,512]{1,0:T(8,128)(2,1)} %collective-permute-done.31.p3), custom_call_target="tpu_custom_call" | custom-call | bytes 4194304 | tf_op jit(solution)/shard_map/pallas_call | solution.py:60
  166.7 3.0 %shard_map.113 = bf16[512,512]{1,0:T(8,128)(2,1)} custom-call(s32[3]{0:T(128)S(1)} %pad_add_fusion.ids.refs_0_, f32[32,1,512]{2,1,0:T(1,128)S(1)} %all-to-all-done.2.refs_1_, f32[32,2,512]{2,1,0:T(2,128)S(1)} %all-to-all-done.stats.refs_2_, bf16[512,512]{1,0:T(8,128)(2,1)S(1)} %copy-done, bf16[2,128,512]{2,1,0:T(8,128)(2,1)S(1)} %copy-done.5, ...), custom_call_target="tpu_custom_call" | custom-call | bytes 4194304 | tf_op jit(solution)/shard_map/pallas_call | solution.py:60
  (103 shorter events, 31.1 us)
Async XLA Ops:
  3.1 9.7 %collective-permute-start.6 = (bf16[512,128]{1,0:T(8,128)(2,1)S(1)}, bf16[512,128]{1,0:T(8,128)(2,1)S(1)}, u32[]{:S(2)}, u32[]{:S(2)}) collective-permute-start(bf16[512,128]{1,0:T(8,128)(2,1)S(1)} %get-tuple-element.70), channel_id=1, source_target_pairs={{0,8},{8,16},{16,24},{24,0},{1,9},{9,17},{17,25},{25,1},{2,10},{10... | collective-permute-start | bytes 393224 | tf_op jit(solution)/shard_map/ppermute | solution.py:486
  4.8 22.2 %collective-permute-start.7 = (bf16[512,128]{1,0:T(8,128)(2,1)S(1)}, bf16[512,128]{1,0:T(8,128)(2,1)S(1)}, u32[]{:S(2)}, u32[]{:S(2)}) collective-permute-start(bf16[512,128]{1,0:T(8,128)(2,1)S(1)} %get-tuple-element.71), channel_id=1, source_target_pairs={{0,16},{8,24},{16,0},{24,8},{1,17},{9,25},{17,1},{25,9},{2,18},{10... | collective-permute-start | bytes 393224 | tf_op jit(solution)/shard_map/ppermute | solution.py:486
  7.7 19.3 %collective-permute-start.8 = (bf16[512,128]{1,0:T(8,128)(2,1)S(1)}, bf16[512,128]{1,0:T(8,128)(2,1)S(1)}, u32[]{:S(2)}, u32[]{:S(2)}) collective-permute-start(bf16[512,128]{1,0:T(8,128)(2,1)S(1)} %get-tuple-element.72), channel_id=1, source_target_pairs={{0,24},{8,0},{16,8},{24,16},{1,25},{9,1},{17,9},{25,17},{2,26},{10... | collective-permute-start | bytes 393224 | tf_op jit(solution)/shard_map/ppermute | solution.py:486
  11.3 23.5 %collective-permute-start.3 = (bf16[512,128]{1,0:T(8,128)(2,1)}, bf16[512,128]{1,0:T(8,128)(2,1)S(1)}, u32[]{:S(2)}, u32[]{:S(2)}) collective-permute-start(bf16[512,128]{1,0:T(8,128)(2,1)} %get-tuple-element.66), channel_id=1, source_target_pairs={{0,8},{8,16},{16,24},{24,0},{1,9},{9,17},{17,25},{25,1},{2,10},{10... | collective-permute-start | bytes 393224 | tf_op jit(solution)/shard_map/ppermute | solution.py:486
  12.0 22.8 %collective-permute-start.4 = (bf16[512,128]{1,0:T(8,128)(2,1)}, bf16[512,128]{1,0:T(8,128)(2,1)S(1)}, u32[]{:S(2)}, u32[]{:S(2)}) collective-permute-start(bf16[512,128]{1,0:T(8,128)(2,1)} %get-tuple-element.67), channel_id=1, source_target_pairs={{0,16},{8,24},{16,0},{24,8},{1,17},{9,25},{17,1},{25,9},{2,18},{10... | collective-permute-start | bytes 393224 | tf_op jit(solution)/shard_map/ppermute | solution.py:486
  12.8 22.0 %collective-permute-start.5 = (bf16[512,128]{1,0:T(8,128)(2,1)}, bf16[512,128]{1,0:T(8,128)(2,1)S(1)}, u32[]{:S(2)}, u32[]{:S(2)}) collective-permute-start(bf16[512,128]{1,0:T(8,128)(2,1)} %get-tuple-element.68), channel_id=1, source_target_pairs={{0,24},{8,0},{16,8},{24,16},{1,25},{9,1},{17,9},{25,17},{2,26},{10... | collective-permute-start | bytes 393224 | tf_op jit(solution)/shard_map/ppermute | solution.py:486
  19.9 14.9 %all-to-all-start = ((f32[32,2,512]{2,1,0:T(2,128)}), f32[32,2,512]{2,1,0:T(2,128)S(1)}, u32[]{:S(2)}, u32[]{:S(2)}) async-start(f32[32,2,512]{2,1,0:T(2,128)} %get-tuple-element.64), calls=%async_computation | async-start | bytes 262144 | tf_op jit(solution)/shard_map/all_to_all | solution.py:495
  27.7 27.6 %collective-permute-start.10 = (bf16[4,4,128,128]{3,2,1,0:T(8,128)(2,1)S(1)}, bf16[4,4,128,128]{3,2,1,0:T(8,128)(2,1)S(1)}, u32[]{:S(2)}, u32[]{:S(2)}) collective-permute-start(bf16[4,4,128,128]{3,2,1,0:T(8,128)(2,1)S(1)} %shard_map.106.v.v0), channel_id=1, source_target_pairs={{0,96},{32,0},{64,32},{96,64},{1,97},{33,1},{65,33},{97,65},{2,98}... | collective-permute-start | bytes 1572872 | tf_op jit(solution)/shard_map/ppermute | solution.py:486
  35.9 21.0 %collective-permute-start.11 = (bf16[4,4,128,128]{3,2,1,0:T(8,128)(2,1)S(1)}, bf16[4,4,128,128]{3,2,1,0:T(8,128)(2,1)S(1)}, u32[]{:S(2)}, u32[]{:S(2)}) collective-permute-start(bf16[4,4,128,128]{3,2,1,0:T(8,128)(2,1)S(1)} %shard_map.104.k.k0), channel_id=1, source_target_pairs={{0,32},{32,64},{64,96},{96,0},{1,33},{33,65},{65,97},{97,1},{2,34}... | collective-permute-start | bytes 1572872 | tf_op jit(solution)/shard_map/ppermute | solution.py:486
  37.9 14.9 %collective-permute-start = (bf16[2,512,128]{2,1,0:T(8,128)(2,1)S(1)}, bf16[2,512,128]{2,1,0:T(8,128)(2,1)S(1)}, u32[]{:S(2)}, u32[]{:S(2)}) collective-permute-start(bf16[2,512,128]{2,1,0:T(8,128)(2,1)S(1)} %copy-done.16), channel_id=1, source_target_pairs={{0,8},{8,16},{16,24},{24,0},{1,9},{9,17},{17,25},{25,1},{2,10},{10... | collective-permute-start | bytes 786440 | tf_op jit(solution)/shard_map/ppermute | solution.py:486
  38.5 18.8 %collective-permute-start.1 = (bf16[2,512,128]{2,1,0:T(8,128)(2,1)S(1)}, bf16[2,512,128]{2,1,0:T(8,128)(2,1)S(1)}, u32[]{:S(2)}, u32[]{:S(2)}) collective-permute-start(bf16[2,512,128]{2,1,0:T(8,128)(2,1)S(1)} %copy-done.14), channel_id=1, source_target_pairs={{0,16},{8,24},{16,0},{24,8},{1,17},{9,25},{17,1},{25,9},{2,18},{10... | collective-permute-start | bytes 786440 | tf_op jit(solution)/shard_map/ppermute | solution.py:486
  40.5 29.7 %collective-permute-start.14 = (bf16[4,4,128,128]{3,2,1,0:T(8,128)(2,1)S(1)}, bf16[4,4,128,128]{3,2,1,0:T(8,128)(2,1)S(1)}, u32[]{:S(2)}, u32[]{:S(2)}) collective-permute-start(bf16[4,4,128,128]{3,2,1,0:T(8,128)(2,1)S(1)} %shard_map.106.v.v0), channel_id=1, source_target_pairs={{0,32},{32,64},{64,96},{96,0},{1,33},{33,65},{65,97},{97,1},{2,34}... | collective-permute-start | bytes 1572872 | tf_op jit(solution)/shard_map/ppermute | solution.py:486
  52.8 17.5 %collective-permute-start.9 = (bf16[4,4,128,128]{3,2,1,0:T(8,128)(2,1)S(1)}, bf16[4,4,128,128]{3,2,1,0:T(8,128)(2,1)S(1)}, u32[]{:S(2)}, u32[]{:S(2)}) collective-permute-start(bf16[4,4,128,128]{3,2,1,0:T(8,128)(2,1)S(1)} %shard_map.104.k.k0), channel_id=1, source_target_pairs={{0,96},{32,0},{64,32},{96,64},{1,97},{33,1},{65,33},{97,65},{2,98}... | collective-permute-start | bytes 1572872 | tf_op jit(solution)/shard_map/ppermute | solution.py:486
  55.3 16.8 %collective-permute-start.13 = (bf16[4,4,128,128]{3,2,1,0:T(8,128)(2,1)S(1)}, bf16[4,4,128,128]{3,2,1,0:T(8,128)(2,1)S(1)}, u32[]{:S(2)}, u32[]{:S(2)}) collective-permute-start(bf16[4,4,128,128]{3,2,1,0:T(8,128)(2,1)S(1)} %collective-permute-done.10.v1), channel_id=1, source_target_pairs={{0,96},{32,0},{64,32},{96,64},{1,97},{33,1},{65,33},{97,65},{2,98}... | collective-permute-start | bytes 1572872 | tf_op jit(solution)/shard_map/ppermute | solution.py:486
  56.9 17.8 %collective-permute-start.12 = (bf16[4,4,128,128]{3,2,1,0:T(8,128)(2,1)S(1)}, bf16[4,4,128,128]{3,2,1,0:T(8,128)(2,1)S(1)}, u32[]{:S(2)}, u32[]{:S(2)}) collective-permute-start(bf16[4,4,128,128]{3,2,1,0:T(8,128)(2,1)S(1)} %collective-permute-done.11.k3), channel_id=1, source_target_pairs={{0,32},{32,64},{64,96},{96,0},{1,33},{33,65},{65,97},{97,1},{2,34}... | collective-permute-start | bytes 1572872 | tf_op jit(solution)/shard_map/ppermute | solution.py:486
  89.9 16.1 %collective-permute-start.25 = (bf16[2,2,4,128,128]{4,3,2,1,0:T(8,128)(2,1)S(1)}, bf16[2,2,4,128,128]{4,3,2,1,0:T(8,128)(2,1)S(1)}, u32[]{:S(2)}, u32[]{:S(2)}) collective-permute-start(bf16[2,2,4,128,128]{4,3,2,1,0:T(8,128)(2,1)S(1)} %get-tuple-element.104), channel_id=1, source_target_pairs={{0,32},{32,64},{64,96},{96,0},{1,33},{33,65},{65,97},{97,1},{2,34}... | collective-permute-start | bytes 1572872 | tf_op jit(solution)/shard_map/ppermute | solution.py:486
  90.0 16.0 %collective-permute-start.26 = (bf16[2,2,4,128,128]{4,3,2,1,0:T(8,128)(2,1)S(1)}, bf16[2,2,4,128,128]{4,3,2,1,0:T(8,128)(2,1)S(1)}, u32[]{:S(2)}, u32[]{:S(2)}) collective-permute-start(bf16[2,2,4,128,128]{4,3,2,1,0:T(8,128)(2,1)S(1)} %get-tuple-element.105), channel_id=1, source_target_pairs={{0,96},{32,0},{64,32},{96,64},{1,97},{33,1},{65,33},{97,65},{2,98}... | collective-permute-start | bytes 1572872 | tf_op jit(solution)/shard_map/ppermute | solution.py:486
  93.2 25.8 %collective-permute-start.18 = (bf16[2,2,4,128,128]{4,3,2,1,0:T(8,128)(2,1)S(1)}, bf16[2,2,4,128,128]{4,3,2,1,0:T(8,128)(2,1)S(1)}, u32[]{:S(2)}, u32[]{:S(2)}) collective-permute-start(bf16[2,2,4,128,128]{4,3,2,1,0:T(8,128)(2,1)S(1)} %get-tuple-element.92), channel_id=1, source_target_pairs={{0,32},{32,64},{64,96},{96,0},{1,33},{33,65},{65,97},{97,1},{2,34}... | collective-permute-start | bytes 1572872 | tf_op jit(solution)/shard_map/ppermute | solution.py:486
  93.2 27.8 %collective-permute-start.19 = (bf16[2,2,4,128,128]{4,3,2,1,0:T(8,128)(2,1)S(1)}, bf16[2,2,4,128,128]{4,3,2,1,0:T(8,128)(2,1)S(1)}, u32[]{:S(2)}, u32[]{:S(2)}) collective-permute-start(bf16[2,2,4,128,128]{4,3,2,1,0:T(8,128)(2,1)S(1)} %get-tuple-element.93), channel_id=1, source_target_pairs={{0,96},{32,0},{64,32},{96,64},{1,97},{33,1},{65,33},{97,65},{2,98}... | collective-permute-start | bytes 1572872 | tf_op jit(solution)/shard_map/ppermute | solution.py:486
  106.1 16.4 %collective-permute-start.27 = (bf16[2,4,128,128]{3,2,1,0:T(8,128)(2,1)S(1)}, bf16[2,4,128,128]{3,2,1,0:T(8,128)(2,1)S(1)}, u32[]{:S(2)}, u32[]{:S(2)}) collective-permute-start(bf16[2,4,128,128]{3,2,1,0:T(8,128)(2,1)S(1)} %get-tuple-element.108), channel_id=1, source_target_pairs={{0,32},{32,64},{64,96},{96,0},{1,33},{33,65},{65,97},{97,1},{2,34}... | collective-permute-start | bytes 786440 | tf_op jit(solution)/shard_map/ppermute | solution.py:486
  106.5 16.1 %collective-permute-start.28 = (bf16[2,4,128,128]{3,2,1,0:T(8,128)(2,1)S(1)}, bf16[2,4,128,128]{3,2,1,0:T(8,128)(2,1)S(1)}, u32[]{:S(2)}, u32[]{:S(2)}) collective-permute-start(bf16[2,4,128,128]{3,2,1,0:T(8,128)(2,1)S(1)} %get-tuple-element.109), channel_id=1, source_target_pairs={{0,96},{32,0},{64,32},{96,64},{1,97},{33,1},{65,33},{97,65},{2,98}... | collective-permute-start | bytes 786440 | tf_op jit(solution)/shard_map/ppermute | solution.py:486
  118.1 17.5 %collective-permute-start.15 = (bf16[3,128,512]{2,1,0:T(8,128)(2,1)S(1)}, bf16[3,128,512]{2,1,0:T(8,128)(2,1)S(1)}, u32[]{:S(2)}, u32[]{:S(2)}) collective-permute-start(bf16[3,128,512]{2,1,0:T(8,128)(2,1)S(1)} %get-tuple-element.86), channel_id=1, source_target_pairs={{0,8},{8,16},{16,24},{24,0},{1,9},{9,17},{17,25},{25,1},{2,10},{10... | collective-permute-start | bytes 1179656 | tf_op jit(solution)/shard_map/ppermute | solution.py:486
  119.0 19.1 %collective-permute-start.16 = (bf16[3,128,512]{2,1,0:T(8,128)(2,1)S(1)}, bf16[3,128,512]{2,1,0:T(8,128)(2,1)S(1)}, u32[]{:S(2)}, u32[]{:S(2)}) collective-permute-start(bf16[3,128,512]{2,1,0:T(8,128)(2,1)S(1)} %get-tuple-element.87), channel_id=1, source_target_pairs={{0,16},{8,24},{16,0},{24,8},{1,17},{9,25},{17,1},{25,9},{2,18},{10... | collective-permute-start | bytes 1179656 | tf_op jit(solution)/shard_map/ppermute | solution.py:486
  121.0 17.5 %collective-permute-start.17 = (bf16[3,128,512]{2,1,0:T(8,128)(2,1)S(1)}, bf16[3,128,512]{2,1,0:T(8,128)(2,1)S(1)}, u32[]{:S(2)}, u32[]{:S(2)}) collective-permute-start(bf16[3,128,512]{2,1,0:T(8,128)(2,1)S(1)} %get-tuple-element.88), channel_id=1, source_target_pairs={{0,24},{8,0},{16,8},{24,16},{1,25},{9,1},{17,9},{25,17},{2,26},{10... | collective-permute-start | bytes 1179656 | tf_op jit(solution)/shard_map/ppermute | solution.py:486
  122.5 8.3 %collective-permute-start.21 = (bf16[2,4,128,128]{3,2,1,0:T(8,128)(2,1)S(1)}, bf16[2,4,128,128]{3,2,1,0:T(8,128)(2,1)S(1)}, u32[]{:S(2)}, u32[]{:S(2)}) collective-permute-start(bf16[2,4,128,128]{3,2,1,0:T(8,128)(2,1)S(1)} %get-tuple-element.97), channel_id=1, source_target_pairs={{0,96},{32,0},{64,32},{96,64},{1,97},{33,1},{65,33},{97,65},{2,98}... | collective-permute-start | bytes 786440 | tf_op jit(solution)/shard_map/ppermute | solution.py:486
  130.1 10.7 %collective-permute-start.29 = (bf16[128,512]{1,0:T(8,128)(2,1)S(1)}, bf16[128,512]{1,0:T(8,128)(2,1)S(1)}, u32[]{:S(2)}, u32[]{:S(2)}) collective-permute-start(bf16[128,512]{1,0:T(8,128)(2,1)S(1)} %get-tuple-element.111), channel_id=1, source_target_pairs={{0,8},{8,16},{16,24},{24,0},{1,9},{9,17},{17,25},{25,1},{2,10},{10... | collective-permute-start | bytes 393224 | tf_op jit(solution)/shard_map/ppermute | solution.py:486
  134.1 32.6 %collective-permute-start.22 = (bf16[2,128,512]{2,1,0:T(8,128)(2,1)}, bf16[2,128,512]{2,1,0:T(8,128)(2,1)S(1)}, u32[]{:S(2)}, u32[]{:S(2)}) collective-permute-start(bf16[2,128,512]{2,1,0:T(8,128)(2,1)} %get-tuple-element.100), channel_id=1, source_target_pairs={{0,8},{8,16},{16,24},{24,0},{1,9},{9,17},{17,25},{25,1},{2,10},{10... | collective-permute-start | bytes 786440 | tf_op jit(solution)/shard_map/ppermute | solution.py:486
  135.6 31.1 %collective-permute-start.23 = (bf16[2,128,512]{2,1,0:T(8,128)(2,1)}, bf16[2,128,512]{2,1,0:T(8,128)(2,1)S(1)}, u32[]{:S(2)}, u32[]{:S(2)}) collective-permute-start(bf16[2,128,512]{2,1,0:T(8,128)(2,1)} %get-tuple-element.101), channel_id=1, source_target_pairs={{0,16},{8,24},{16,0},{24,8},{1,17},{9,25},{17,1},{25,9},{2,18},{10... | collective-permute-start | bytes 786440 | tf_op jit(solution)/shard_map/ppermute | solution.py:486
  138.1 28.6 %collective-permute-start.24 = (bf16[2,128,512]{2,1,0:T(8,128)(2,1)}, bf16[2,128,512]{2,1,0:T(8,128)(2,1)}, u32[]{:S(2)}, u32[]{:S(2)}) collective-permute-start(bf16[2,128,512]{2,1,0:T(8,128)(2,1)} %get-tuple-element.102), channel_id=1, source_target_pairs={{0,24},{8,0},{16,8},{24,16},{1,25},{9,1},{17,9},{25,17},{2,26},{10... | collective-permute-start | bytes 786440 | tf_op jit(solution)/shard_map/ppermute | solution.py:486
  138.5 24.1 %collective-permute-start.30 = (bf16[128,512]{1,0:T(8,128)(2,1)}, bf16[128,512]{1,0:T(8,128)(2,1)}, u32[]{:S(2)}, u32[]{:S(2)}) collective-permute-start(bf16[128,512]{1,0:T(8,128)(2,1)} %get-tuple-element.112), channel_id=1, source_target_pairs={{0,16},{8,24},{16,0},{24,8},{1,17},{9,25},{17,1},{25,9},{2,18},{10... | collective-permute-start | bytes 393224 | tf_op jit(solution)/shard_map/ppermute | solution.py:486
  141.5 21.2 %collective-permute-start.31 = (bf16[128,512]{1,0:T(8,128)(2,1)}, bf16[128,512]{1,0:T(8,128)(2,1)}, u32[]{:S(2)}, u32[]{:S(2)}) collective-permute-start(bf16[128,512]{1,0:T(8,128)(2,1)} %get-tuple-element.113), channel_id=1, source_target_pairs={{0,24},{8,0},{16,8},{24,16},{1,25},{9,1},{17,9},{25,17},{2,26},{10... | collective-permute-start | bytes 393224 | tf_op jit(solution)/shard_map/ppermute | solution.py:486
  155.4 11.3 %all-to-all-start.2 = ((f32[32,1,512]{2,1,0:T(1,128)}), f32[32,1,512]{2,1,0:T(1,128)S(1)}, u32[]{:S(2)}, u32[]{:S(2)}) async-start(f32[32,1,512]{2,1,0:T(1,128)} %copy-done.8), calls=%async_computation.2 | async-start | bytes 131072 | tf_op jit(solution)/shard_map/all_to_all | solution.py:495
  (26 other events, 157.7 us)
